TPU v7x, 256 devices: a whole 4x4x8 slice. The times are simulated.
256 devices in a mesh: row: 16 (over x_lo, y, core), col: 16 (over z, x_hi).
Axes of the slice: x: 4 (x_hi: 2, x_lo: 2; x = x_hi * 2 + x_lo), y: 4, z: 8, core: 2. Of those that a mesh axis runs over, the one named last changes fastest.
Arguments:
- images: bfloat16 [2, 64, 64, 2048], P(None, 'row', None, 'col'), may hold values from -6 to 6
- dw_kernel: float32 [7, 7, 2048], P(None, None, 'col'), may hold values from -3 to 3
- norm_gain: float32 [2048], P('col'), may hold values from 0.5 to 1.5
- proj_in: bfloat16 [2048, 8192], P('row', 'col'), may hold values from -0.125 to 0.125
- proj_out: bfloat16 [2048, 8192], P('row', 'col'), may hold values from -0.0625 to 0.0625
- layer_scale: float32 [2048], P('col'), may hold values from 0.1 to 1.9
- cotangent: bfloat16 [2, 64, 64, 2048], P(None, 'row', None, 'col'), may hold values from -0.59765625 to 0.59765625
Outputs:
- block_out: bfloat16 [2, 64, 64, 2048], P(None, 'row', None, 'col')
- grad_images: bfloat16 [2, 64, 64, 2048], P(None, 'row', None, 'col')
- grad_proj_in: bfloat16 [2048, 8192], P('row', 'col')
- grad_proj_out: bfloat16 [2048, 8192], P('row', 'col')
All inputs are finite; a program needn't handle non-finite values.
Results may differ from a plain program's by a relative error of at most 0.023.
Values may be sent and summed in bfloat16 or wider, within the bound.
A program may use at most 64 MiB of HBM per device.

v0:
```python
import jax
import jax.numpy as jnp
from jax import lax
from jax.sharding import PartitionSpec as P

C = 2048
KS = 7


def with_halo(block, sides, width):
    for axis, dim in sides:
        count = lax.axis_size(axis)
        forward = [(i, i + 1) for i in range(count - 1)]
        backward = [(target, source) for source, target in forward]
        low = lax.ppermute(
            lax.slice_in_dim(block, block.shape[dim] - width, None, axis=dim), axis, forward
        )
        high = lax.ppermute(lax.slice_in_dim(block, 0, width, axis=dim), axis, backward)
        block = jnp.concatenate([low, block, high], axis=dim)
    return block


def taps_sum(padded, dw_kernel, img_rows, img_cols, flipped):
    total = jnp.zeros(padded.shape[:1] + (img_rows, img_cols) + padded.shape[3:], jnp.float32)
    reach = 2 * (KS // 2)
    for tap_row in range(KS):
        for tap_col in range(KS):
            off_row = reach - tap_row if flipped else tap_row
            off_col = reach - tap_col if flipped else tap_col
            total = (
                total
                + dw_kernel[tap_row, tap_col]
                * padded[:, off_row : off_row + img_rows, off_col : off_col + img_cols, :]
            )
    return total


def gelu_slope(values):
    return (
        0.5 * (1.0 + lax.erf(values * 0.7071067811865476))
        + values * jnp.exp(-0.5 * values * values) * 0.3989422804014327
    )


def on_device(images, dw_kernel, norm_gain, proj_in, proj_out, layer_scale, cotangent):
    img_batch, strip_rows, img_cols, local_ch = images.shape
    pixels = img_batch * strip_rows * img_cols
    reach = KS // 2
    contract_last = (((1,), (1,)), ((), ()))
    contract_first = (((0,), (0,)), ((), ()))
    rimmed = with_halo(images, (("row", 1),), reach)
    padded = jnp.pad(rimmed.astype(jnp.float32), ((0, 0), (0, 0), (reach, reach), (0, 0)))
    conv_out = taps_sum(padded, dw_kernel, strip_rows, img_cols, False).reshape(pixels, local_ch)
    row_mean = lax.psum(jnp.sum(conv_out, axis=1), "col") / C
    centred = conv_out - row_mean[:, None]
    row_var = lax.psum(jnp.sum(centred * centred, axis=1), "col") / C
    inv_std = lax.rsqrt(row_var + 1e-06)
    normed = centred * inv_std[:, None]
    scaled = (normed * norm_gain).astype(jnp.bfloat16)
    full_in = lax.all_gather(scaled, "col", axis=1, tiled=True)
    in_panel = lax.all_gather(proj_in, "row", axis=0, tiled=True)
    out_panel = lax.all_gather(proj_out, "row", axis=0, tiled=True)
    hidden_pre = jnp.dot(full_in, in_panel, preferred_element_type=jnp.float32)
    hidden = jax.nn.gelu(hidden_pre, approximate=False).astype(jnp.bfloat16)
    contrib = lax.dot_general(hidden, out_panel, contract_last, preferred_element_type=jnp.float32)
    branch = lax.psum_scatter(
        contrib.astype(jnp.bfloat16), "col", scatter_dimension=1, tiled=True
    ).astype(jnp.float32)
    residual_in = images.reshape(pixels, local_ch).astype(jnp.float32)
    block_out = (residual_in + layer_scale * branch).astype(jnp.bfloat16).reshape(images.shape)
    cot_flat = cotangent.reshape(pixels, local_ch).astype(jnp.float32)
    grad_branch = (cot_flat * layer_scale).astype(jnp.bfloat16)
    full_grad = lax.all_gather(grad_branch, "col", axis=1, tiled=True)
    grad_proj_out = lax.psum_scatter(
        lax.dot_general(
            full_grad, hidden, contract_first, preferred_element_type=jnp.float32
        ).astype(jnp.bfloat16),
        "row",
        scatter_dimension=0,
        tiled=True,
    )
    grad_hidden = jnp.dot(full_grad, out_panel, preferred_element_type=jnp.float32)
    grad_pre = (grad_hidden * gelu_slope(hidden_pre)).astype(jnp.bfloat16)
    grad_proj_in = lax.psum_scatter(
        lax.dot_general(
            full_in, grad_pre, contract_first, preferred_element_type=jnp.float32
        ).astype(jnp.bfloat16),
        "row",
        scatter_dimension=0,
        tiled=True,
    )
    back_part = lax.dot_general(
        grad_pre, in_panel, contract_last, preferred_element_type=jnp.float32
    )
    grad_scaled = lax.psum_scatter(
        back_part.astype(jnp.bfloat16), "col", scatter_dimension=1, tiled=True
    ).astype(jnp.float32)
    weighted = grad_scaled * norm_gain
    sum_one, sum_two = lax.psum(
        (jnp.sum(weighted, axis=1), jnp.sum(weighted * normed, axis=1)), "col"
    )
    grad_conv = inv_std[:, None] * (weighted - sum_one[:, None] / C - normed * sum_two[:, None] / C)
    grad_conv = grad_conv.reshape(img_batch, strip_rows, img_cols, local_ch)
    grad_rim = with_halo(grad_conv.astype(jnp.bfloat16), (("row", 1),), reach).astype(
        grad_conv.dtype
    )
    grad_pad = jnp.pad(grad_rim, ((0, 0), (0, 0), (reach, reach), (0, 0)))
    input_grad = taps_sum(grad_pad, dw_kernel, strip_rows, img_cols, True)
    grad_images = (cotangent.astype(jnp.float32) + input_grad).astype(jnp.bfloat16)
    return (block_out, grad_images, grad_proj_in, grad_proj_out)


def solution(mesh):
    placed = (
        P(None, "row", None, "col"),
        P(None, None, "col"),
        P("col"),
        P("row", "col"),
        P("row", "col"),
        P("col"),
        P(None, "row", None, "col"),
    )
    return jax.shard_map(
        on_device,
        mesh=mesh,
        in_specs=placed,
        out_specs=(
            P(None, "row", None, "col"),
            P(None, "row", None, "col"),
            P("row", "col"),
            P("row", "col"),
        ),
        check_vma=False,
    )
```

profile of v0, /device:TPU:2, one launch (start us, length us, event | category | flops | bytes accessed | tf_op | source)
XLA Modules:
  0.0 874.4 jit_solution(5250566784383177505)
XLA Ops:
  7.2 0.7 all-gather.7.cloned.1.call-update
  7.9 1.0 fusion.204
  8.9 1.9 collective-permute-start
  10.9 5.8 collective-permute-start.1
  16.6 1.0 slice_bitcast_fusion.48
  17.6 1.0 slice_bitcast_fusion.47
  18.6 0.9 slice_bitcast_fusion.46
  19.5 1.0 maximum_convert_fusion
  20.5 1.8 fusion.201
  22.3 0.1 reduce_sum.41
  22.4 44.0 %psum.28 = f32[512]{0:T(512)S(1)} all-reduce(f32[512]{0:T(512)S(1)} %reduce_sum.41), channel_id=1, replica_groups=mesh['row'=16,'col'=16] {'col'}, use_global_device_ids=true, to_apply=%region_1.2 | all-reduce | flops 512 | bytes 4096 | tf_op jit(solution)/shard_map/psum | solution.py:54
  66.4 0.1 sub.28
  66.5 0.3 multiply_reduce_fusion.1
  66.8 0.1 reduce_sum.43
  66.9 36.6 %psum.29 = f32[512]{0:T(512)S(1)} all-reduce(f32[512]{0:T(512)S(1)} %reduce_sum.43), channel_id=1, replica_groups=mesh['row'=16,'col'=16] {'col'}, use_global_device_ids=true, to_apply=%region_3.4 | all-reduce | flops 512 | bytes 4096 | tf_op jit(solution)/shard_map/psum | solution.py:56
  103.5 0.9 multiply_convert_fusion.1
  104.4 0.7 all-gather.9.cloned.1.call-update
  105.2 80.3 %all-gather.5.cloned.1.call-done = bf16[512,2048]{1,0:T(8,128)(2,1)} async-done(((bf16[512,128]{1,0:T(8,128)(2,1)}), bf16[512,2048]{1,0:T(8,128)(2,1)}) %all-gather.5.cloned.1.call-update) | async-done | bytes 2097168 | tf_op jit(solution)/shard_map/all_gather | solution.py:60
  185.5 6.5 fusion.3
  192.0 29.1 %all-gather.9.cloned.1.call-done = bf16[2048,512]{1,0:T(8,128)(2,1)} async-done(((bf16[128,512]{1,0:T(8,128)(2,1)}), bf16[2048,512]{1,0:T(8,128)(2,1)}) %all-gather.9.cloned.1.call-update) | async-done | bytes 2097168 | tf_op jit(solution)/shard_map/all_gather | solution.py:62
  221.1 2.9 convolution_convert_fusion.3
  224.1 2.5 copy.11
  226.7 207.3 %reduce-scatter.13.cloned.1.call-done = bf16[128,512]{1,0:T(8,128)(2,1)} async-done(((bf16[2048,512]{1,0:T(8,128)(2,1)}), bf16[128,512]{1,0:T(8,128)(2,1)}) %reduce-scatter.13.cloned.1.call-update) | async-done | bytes 131088
  434.0 1.0 copy.12
  435.0 0.8 fusion.198
  435.9 83.9 %all-gather.11.cloned.1.call-done = bf16[512,2048]{1,0:T(8,128)(2,1)} async-done(((bf16[512,128]{1,0:T(8,128)(2,1)}), bf16[512,2048]{1,0:T(8,128)(2,1)}) %all-gather.11.cloned.1.call-update) | async-done | bytes 2097168 | tf_op jit(solution)/shard_map/all_gather | solution.py:73
  519.8 3.5 fusion
  523.3 0.8 copy-done.8
  524.1 1.3 convolution_convert_fusion.2
  525.4 2.5 copy.13
  528.0 1.5 copy-done.5
  529.5 3.7 convolution_convert_fusion.1
  533.2 0.2 reduce-scatter.11.cloned.1.call-start
  533.4 1.3 copy-done.7
  534.8 2.6 convolution_convert_fusion
  537.4 195.2 %reduce-scatter.15.cloned.1.call-done = bf16[128,512]{1,0:T(8,128)(2,1)} async-done(((bf16[2048,512]{1,0:T(8,128)(2,1)}), bf16[128,512]{1,0:T(8,128)(2,1)}) %reduce-scatter.15.cloned.1.call-update) | async-done | bytes 131088
  732.7 1.0 copy.14
  733.7 0.4 fusion.200
  734.1 39.3 %all-reduce.2 = (f32[512]{0:T(512)S(1)}, f32[512]{0:T(512)S(1)}) all-reduce(f32[512]{0:T(512)S(1)} %get-tuple-element.5, f32[512]{0:T(512)S(1)} %get-tuple-element.4), channel_id=1, replica_groups=mesh['row'=16,'col'=16] {'col'}, use_global_device_ids=true, to_apply=%region_9.10 | all-reduce | flops 1024 | bytes 8192 | tf_op jit(solution)/shard_map/psum | solution.py:99
  773.3 0.3 multiply_convert_fusion
  773.7 1.9 collective-permute-start.2
  775.6 5.8 collective-permute-start.3
  781.4 0.6 collective-permute-done.2
  782.0 1.7 collective-permute-done.3
  783.7 0.1 maximum_convert_fusion.1
  783.7 2.4 fusion.192
  786.1 13.8 %reduce-scatter.9.cloned.1.call-done = bf16[128,512]{1,0:T(8,128)(2,1)} async-done(((bf16[2048,512]{1,0:T(8,128)(2,1)}), bf16[128,512]{1,0:T(8,128)(2,1)}) %reduce-scatter.9.cloned.1.call-update) | async-done | bytes 131088 | tf_op jit(solution)/shard_map/reduce_scatter | solution.py:84
  800.0 67.6 %reduce-scatter.11.cloned.1.call-done = bf16[128,512]{1,0:T(8,128)(2,1)} async-done(((bf16[2048,512]{1,0:T(8,128)(2,1)}), bf16[128,512]{1,0:T(8,128)(2,1)}) %reduce-scatter.11.cloned.1.call-update) | async-done | bytes 131088 | tf_op jit(solution)/shard_map/reduce_scatter | solution.py:74
  (35 shorter events, 0.5 us)
Async XLA Ops:
  7.2 98.0 %all-gather.7.cloned.1.call-start = ((), (), s32[]{:S(2)}) async-start(), calls=%async_computation.5 | async-start | bytes 2228224 | tf_op jit(solution)/shard_map/all_gather | solution.py:61
  7.9 177.6 %all-gather.5.cloned.1.call-start = ((), (), s32[]{:S(2)}) async-start(), calls=%async_computation.4 | async-start | bytes 2228224 | tf_op jit(solution)/shard_map/all_gather | solution.py:60
  8.9 10.6 %collective-permute-start = (bf16[2,3,64,128]{3,2,1,0:T(8,128)(2,1)S(1)}, bf16[2,3,64,128]{3,2,1,0:T(8,128)(2,1)S(1)}, u32[]{:S(2)}, u32[]{:S(2)}) collective-permute-start(bf16[2,3,64,128]{3,2,1,0:T(8,128)(2,1)S(1)} %get-tuple-element.12), channel_id=1, source_target_pairs={{0,16},{16,32},{32,48},{48,64},{64,80},{80,96},{96,112},{112,128},... | collective-permute-start | bytes 294920 | tf_op jit(solution)/shard_map/ppermute | solution.py:15
  10.9 8.7 collective-permute-start.1
  17.6 85.9 %copy-start.2 = (f32[128]{0:T(128)S(1)}, f32[128]{0:T(128)}, u32[]{:S(2)}) copy-start(f32[128]{0:T(128)} %param.9) | copy-start | bytes 1540
  104.4 116.8 %all-gather.9.cloned.1.call-start = ((), (), s32[]{:S(2)}) async-start(), calls=%async_computation.6 | async-start | bytes 2228224 | tf_op jit(solution)/shard_map/all_gather | solution.py:62
  105.1 328.9 %reduce-scatter.13.cloned.1.call-start = ((), (), s32[]{:S(2)}) async-start(), calls=%async_computation.10 | async-start | bytes 2228224
  226.6 208.4 %copy-start = (bf16[2,4,64,128]{3,2,1,0:T(8,128)(2,1)S(1)}, bf16[2,4,64,128]{3,2,1,0:T(8,128)(2,1)}, u32[]{:S(2)}) copy-start(bf16[2,4,64,128]{3,2,1,0:T(8,128)(2,1)} %param.7) | copy-start | bytes 393220
  226.6 208.4 %copy-start.1 = (bf16[2,4,64,128]{3,2,1,0:T(8,128)(2,1)S(1)}, bf16[2,4,64,128]{3,2,1,0:T(8,128)(2,1)}, u32[]{:S(2)}) copy-start(bf16[2,4,64,128]{3,2,1,0:T(8,128)(2,1)} %param.13) | copy-start | bytes 393220
  226.6 208.4 %copy-start.3 = (f32[128]{0:T(128)S(1)}, f32[128]{0:T(128)}, u32[]{:S(2)}) copy-start(f32[128]{0:T(128)} %param.12) | copy-start | bytes 1540
  226.6 293.2 %copy-start.6 = (bf16[2048,512]{1,0:T(8,128)(2,1)S(1)}, bf16[2048,512]{1,0:T(8,128)(2,1)}, u32[]{:S(2)}) copy-start(bf16[2048,512]{1,0:T(8,128)(2,1)} %all-gather.9.cloned.1.call-done) | copy-start | bytes 6291460
  226.7 293.2 %all-gather.11.cloned.1.call-start = ((), (), s32[]{:S(2)}) async-start(), calls=%async_computation.7 | async-start | bytes 2228224 | tf_op jit(solution)/shard_map/all_gather | solution.py:73
  435.8 296.8 %reduce-scatter.15.cloned.1.call-start = ((), (), s32[]{:S(2)}) async-start(), calls=%async_computation.11 | async-start | bytes 2228224
  519.8 4.3 copy-start.4
  523.3 0.8 copy-start.8
  527.9 1.6 copy-start.5
  528.0 272.0 %reduce-scatter.9.cloned.1.call-start = ((), (), s32[]{:S(2)}) async-start(), calls=%async_computation.8 | async-start | bytes 2228224 | tf_op jit(solution)/shard_map/reduce_scatter | solution.py:84
  533.2 1.6 copy-start.7
  533.2 334.4 %reduce-scatter.11.cloned.1.call-start = ((), (), s32[]{:S(2)}) async-start(), calls=%async_computation.9 | async-start | bytes 2228224 | tf_op jit(solution)/shard_map/reduce_scatter | solution.py:74
  773.7 8.3 collective-permute-start.2
  775.6 8.0 collective-permute-start.3
Sparse Core Ops, SparseCore 0:
  9.8 39.1 all-gather.6
  104.5 80.9 all-gather.4
  187.4 33.7 all-gather.8
  226.8 207.1 reduce-scatter.12
  436.9 82.9 all-gather.10
  528.1 204.5 reduce-scatter.14
  735.8 64.1 reduce-scatter.8
  803.1 64.4 reduce-scatter.10
where the time goes:
time: 876 us; the launch traced here: 874 us
  waiting for transfers between devices  681 us (78%)
  blocking collectives  120 us (14%)
  matrix products  20.5 us (2%)
  starting transfers between devices  15.8 us (2%)
  local copies, waits for them, and re-layouts  14.9 us (2%)
  between operations  14.3 us (2%)
    unnamed x10, waiting for transfers between devices  404 us
    all_gather x1, waiting for transfers between devices, on_device(): full_grad = lax.all_gather(grad_branch, 'col', axis=1, tiled=True)  83.9 us
    all_gather x1, waiting for transfers between devices, on_device(): full_in = lax.all_gather(scaled, 'col', axis=1, tiled=True)  80.3 us
    reduce_scatter x1, waiting for transfers between devices, on_device(): lax.psum_scatter(lax.dot_general(full_grad, hidden, contract_first, prefe...  67.6 us
    psum x1, blocking collectives, on_device(): row_mean = lax.psum(jnp.sum(conv_out, axis=1), 'col') / C  44 us
    psum x1, blocking collectives, on_device(): lax.psum((jnp.sum(weighted, axis=1), jnp.sum(weighted * normed, axis=1)),...  39.3 us
    psum x1, blocking collectives, on_device(): row_var = lax.psum(jnp.sum(centred * centred, axis=1), 'col') / C  36.6 us
    all_gather x1, waiting for transfers between devices, on_device(): out_panel = lax.all_gather(proj_out, 'row', axis=0, tiled=True)  29.1 us
  transfers between devices with their start and end apart: 12, of which 9 were waited for; matrix products, arithmetic and copies ran while one was open for 3% of the time, Pallas kernels for 0%

commit v1 on v0

v1 whole, which is shorter than its diff:
```python
import functools

import jax
import jax.numpy as jnp
from jax import lax
from jax.experimental import pallas as pl
from jax.experimental.pallas import tpu as pltpu
from jax.sharding import PartitionSpec as P

MESH = pl.DeviceIdType.MESH
F32, BF16 = jnp.float32, jnp.bfloat16
C = 2048
KS = 7
NZ, NY = 8, 4
CB = 128
HB = 512
PIX = 512
LEFT = 8
TAP0 = LEFT - KS // 2
N_SEMS = 256
CONTRACT_LAST = (((1,), (1,)), ((), ()))
CONTRACT_FIRST = (((0,), (0,)), ((), ()))


def kernel(
    n0,
    images, dwk, gain, w_in, w_out, lscale, cot,
    block_out, grad_images, gp_in, gp_out,
    pad, halo_lo, halo_hi, ghalo_lo, ghalo_hi, edge_lo, edge_hi,
    conv, normed, istd, tmp, st1, st2,
    xg, gg, wi, wo, hp, gh, hid, gpre,
    cb, bk, cb_m, cb_p, bk_m, bk_p, cb_m1, cb_p1, bk_m1, bk_p1,
    cb_x, bk_x, cb_xs, bk_xs, cb_xr, bk_xr, gs,
    g1, g2, g1_c, g2_c, g1_m, g1_p, g2_m, g2_p, g1_r, g2_r,
    send_sem, recv_sem,
):
    n1 = PIX - n0
    row, col = lax.axis_index("row"), lax.axis_index("col")
    xlo, y, core = row // 8, (row // 2) % NY, row % 2
    z, xhi = col // 2, col % 2

    def at_z(step):
        return (z + step + NZ) % NZ

    def at_y(step):
        return (y + step + NY) % NY

    z_up = {"row": row, "col": at_z(1) * 2 + xhi}
    z_down = {"row": row, "col": at_z(-1) * 2 + xhi}
    x_far = {"row": row, "col": z * 2 + (1 - xhi)}
    y_up = {"row": xlo * 8 + at_y(1) * 2 + core, "col": col}
    y_down = {"row": xlo * 8 + at_y(-1) * 2 + core, "col": col}
    x_near = {"row": (1 - xlo) * 8 + y * 2 + core, "col": col}
    sibling = {"row": xlo * 8 + y * 2 + (1 - core), "col": col}
    strip_up = {"row": (row + 1) % 16, "col": col}
    strip_down = {"row": (row + 15) % 16, "col": col}

    def col_peer(step):
        return {"row": row, "col": (col + step) % 16}

    started = []

    def send(src, dst, where):
        index = len(started)
        copy = pltpu.make_async_remote_copy(
            src_ref=src, dst_ref=dst, send_sem=send_sem.at[index], recv_sem=recv_sem.at[index],
            device_id=where, device_id_type=MESH,
        )
        copy.start()
        started.append(copy)
        return copy

    barrier = pltpu.get_barrier_semaphore()
    peers = [strip_up, strip_down, y_up, y_down, x_near] + [col_peer(k) for k in range(1, 16)]
    for peer in peers:
        pl.semaphore_signal(barrier, inc=1, device_id=peer, device_id_type=MESH)
    pl.semaphore_wait(barrier, len(peers))

    def ring_gather(buf, half, first, count):
        def block(zi, lo=0, n=count):
            return buf.at[zi, half, pl.ds(first + lo, n)]
        up = send(block(z), block(z), z_up)
        down = send(block(z), block(z), z_down)
        yield
        for k in (1, 2, 3):
            up.wait_recv()
            down.wait_recv()
            if k < 3:
                up = send(block(at_z(-k)), block(at_z(-k)), z_up)
                down = send(block(at_z(k)), block(at_z(k)), z_down)
            else:
                h = count // 2
                up = send(block(at_z(-3), 0, h), block(at_z(-3), 0, h), z_up)
                down = send(block(at_z(3), h, h), block(at_z(3), h, h), z_down)
            yield
        up.wait_recv()
        down.wait_recv()
        yield

    def gather_col(buf):
        def rows(zi, half, first, count):
            return buf.at[zi, half, pl.ds(first, count)]
        waits = {k: [] for k in range(5)}
        rings = []
        if n0:
            far = send(rows(z, xhi, 0, n0), rows(z, xhi, 0, n0), x_far)
            ring = ring_gather(buf, xhi, 0, n0)
            next(ring)
            rings.append(ring)
        if n1:
            ring1 = ring_gather(buf, xhi, n0, n1)
            next(ring1)
            waits[0].append(send(rows(z, xhi, n0, n1), rows(z, xhi, n0, n1), x_far))
        yield
        if n0:
            far.wait_recv()
            ring = ring_gather(buf, 1 - xhi, 0, n0)
            next(ring)
            rings.append(ring)
        yield
        for k in (1, 2, 3, 4):
            if n1:
                next(ring1)
                for step in sorted({-k, k} if k < 4 else {4}):
                    part = rows(at_z(step), xhi, n0, n1)
                    waits[k].append(send(part, part, x_far))
            for ring in rings:
                next(ring)
            if k == 1:
                for copy in waits[0]:
                    copy.wait_recv()
            if k > 1:
                for copy in waits[k - 1]:
                    copy.wait_recv()
            yield
        for copy in waits[4]:
            copy.wait_recv()
        yield

    def gather_row(buf, own):
        def block(k, yi, xi, lo=0, n=CB):
            return buf.at[k, yi, xi, pl.ds(lo, n)]
        waits = []

        def share(yi, xi):
            waits.append(send(block(core, yi, xi), block(core, yi, xi), sibling))

        buf[core, y, xlo] = own[...]
        near = send(own, block(core, y, xlo), x_near)
        up, down = {}, {}
        up[0] = send(own, block(core, y, xlo), y_up)
        down[0] = send(own, block(core, y, xlo), y_down)
        waits.append(send(own, block(core, y, xlo), sibling))
        yield
        near.wait_recv()
        other = 1 - xlo
        up[1] = send(block(core, y, other), block(core, y, other), y_up)
        down[1] = send(block(core, y, other), block(core, y, other), y_down)
        share(y, other)
        yield
        h = CB // 2
        for i, xi in enumerate((xlo, other)):
            up[i].wait_recv()
            down[i].wait_recv()
            low, high = block(core, at_y(-1), xi, 0, h), block(core, at_y(1), xi, h, h)
            up[i] = send(low, low, y_up)
            down[i] = send(high, high, y_down)
            share(at_y(-1), xi)
            share(at_y(1), xi)
            yield
        for i, xi in enumerate((xlo, other)):
            up[i].wait_recv()
            down[i].wait_recv()
            share(at_y(2), xi)
        yield
        for copy in waits:
            copy.wait_recv()
        yield

    def add_into(dst, src):
        dst[...] = (dst[...].astype(F32) + src[...].astype(F32)).astype(BF16)

    def scatter_col(buf, rm, rp, rm1, rp1, rx1, xs, xr, total):
        h0, h1 = n0 // 2, n1 // 2
        if n1:
            first = {}
            for step in (4, -3, 3, -2, 2, -1, 1, 0):
                first[step] = send(
                    buf.at[at_z(step), 1 - xhi, pl.ds(n0, n1)], rx1.at[at_z(step)], x_far
                )
        copies = {}

        def block0(zi, lo=0, n=n0):
            return buf.at[zi, :, pl.ds(lo, n)]

        def block1(zi, lo=0, n=n1):
            return buf.at[zi, xhi, pl.ds(n0 + lo, n)]

        for k in (1, 2, 3, 4):
            dist = 5 - k
            if n0:
                if k == 1:
                    down = send(block0(at_z(-4), 0, h0), rm.at[0, :, pl.ds(0, h0)], z_down)
                    up = send(block0(at_z(4), h0, h0), rp.at[0, :, pl.ds(0, h0)], z_up)
                else:
                    down.wait_recv()
                    if k == 2:
                        add_into(block0(at_z(-dist), 0, h0), rm.at[0, :, pl.ds(0, h0)])
                    else:
                        add_into(block0(at_z(-dist)), rm.at[k - 2])
                    down = send(block0(at_z(-dist)), rm.at[k - 1], z_down)
                    up.wait_recv()
                    if k == 2:
                        add_into(block0(at_z(dist), h0, h0), rp.at[0, :, pl.ds(0, h0)])
                    else:
                        add_into(block0(at_z(dist)), rp.at[k - 2])
                    up = send(block0(at_z(dist)), rp.at[k - 1], z_up)
            if n1:
                if k == 1:
                    first[4].wait_recv()
                    add_into(block1(at_z(4)), rx1.at[at_z(4)])
                    down1 = send(block1(at_z(-4), 0, h1), rm1.at[0, pl.ds(0, h1)], z_down)
                    up1 = send(block1(at_z(4), h1, h1), rp1.at[0, pl.ds(0, h1)], z_up)
                else:
                    first[-dist].wait_recv()
                    add_into(block1(at_z(-dist)), rx1.at[at_z(-dist)])
                    first[dist].wait_recv()
                    add_into(block1(at_z(dist)), rx1.at[at_z(dist)])
                    down1.wait_recv()
                    if k == 2:
                        add_into(block1(at_z(-dist), 0, h1), rm1.at[0, pl.ds(0, h1)])
                    else:
                        add_into(block1(at_z(-dist)), rm1.at[k - 2])
                    down1 = send(block1(at_z(-dist)), rm1.at[k - 1], z_down)
                    up1.wait_recv()
                    if k == 2:
                        add_into(block1(at_z(dist), h1, h1), rp1.at[0, pl.ds(0, h1)])
                    else:
                        add_into(block1(at_z(dist)), rp1.at[k - 2])
                    up1 = send(block1(at_z(dist)), rp1.at[k - 1], z_up)
            yield
        if n0:
            down.wait_recv()
            up.wait_recv()
            theirs = 1 - xhi
            xs[...] = (
                buf[z, theirs, 0:n0].astype(F32)
                + rm[3, theirs].astype(F32)
                + rp[3, theirs].astype(F32)
            ).astype(BF16)
            far = send(xs, xr, x_far)
        if n1:
            first[0].wait_recv()
            down1.wait_recv()
            up1.wait_recv()
            total[n0:PIX] = (
                buf[z, xhi, n0:PIX].astype(F32)
                + rx1[z].astype(F32)
                + rm1[3].astype(F32)
                + rp1[3].astype(F32)
            )
        yield
        if n0:
            far.wait_recv()
            total[0:n0] = (
                buf[z, xhi, 0:n0].astype(F32)
                + rm[3, xhi].astype(F32)
                + rp[3, xhi].astype(F32)
                + xr[...].astype(F32)
            )
        yield

    def scatter_row(buf, rc, rm, rp, rx, xs_slot, out):
        h = CB // 2
        shared = {}
        for step in (2, -1, 1, 0):
            shared[step] = send(buf.at[1 - core, at_y(step)], rc.at[at_y(step)], sibling)
        yield
        shared[2].wait_recv()
        add_into(buf.at[core, at_y(2)], rc.at[at_y(2)])
        down = send(
            buf.at[core, at_y(-2), :, pl.ds(0, h)], rm.at[0, :, pl.ds(0, h)], y_down
        )
        up = send(buf.at[core, at_y(2), :, pl.ds(h, h)], rp.at[0, :, pl.ds(0, h)], y_up)
        for step in (-1, 1, 0):
            shared[step].wait_recv()
            add_into(buf.at[core, at_y(step)], rc.at[at_y(step)])
        yield
        down.wait_recv()
        add_into(buf.at[core, at_y(-1), :, pl.ds(0, h)], rm.at[0, :, pl.ds(0, h)])
        down = send(buf.at[core, at_y(-1)], rm.at[1], y_down)
        up.wait_recv()
        add_into(buf.at[core, at_y(1), :, pl.ds(h, h)], rp.at[0, :, pl.ds(0, h)])
        up = send(buf.at[core, at_y(1)], rp.at[1], y_up)
        yield
        down.wait_recv()
        up.wait_recv()
        theirs = 1 - xlo
        xs_slot[0] = (
            buf[core, y, theirs].astype(F32)
            + rm[1, theirs].astype(F32)
            + rp[1, theirs].astype(F32)
        ).astype(BF16)
        near = send(xs_slot.at[0], rx.at[1], x_near)
        yield
        near.wait_recv()
        out[...] = (
            buf[core, y, xlo].astype(F32)
            + rm[1, xlo].astype(F32)
            + rp[1, xlo].astype(F32)
            + rx[1].astype(F32)
        ).astype(BF16)
        yield

    def taps_sum(flipped, finish):
        def strip_row(bh, carry):
            image, line = bh // 4, bh % 4
            total = jnp.zeros((64, CB), F32)
            for i in range(KS):
                for j in range(KS):
                    tap = dwk[KS - 1 - i, pl.ds(KS - 1 - j, 1)] if flipped else dwk[i, pl.ds(j, 1)]
                    total = total + tap * pad[image, line + i, pl.ds(TAP0 + j, 64)]
            finish(bh, total)
            return carry

        lax.fori_loop(0, 8, strip_row, 0)

    def set_halo(low, high):
        pad[:, 0:3, LEFT : LEFT + 64] = jnp.where(row > 0, low[...].astype(F32), 0.0)
        pad[:, 7:10, LEFT : LEFT + 64] = jnp.where(row < 15, high[...].astype(F32), 0.0)

    lane = lax.broadcasted_iota(jnp.int32, (64, CB), 1)

    def put_sums(bh, first, second):
        tmp[pl.ds(pl.multiple_of(bh * 64, 64), 64)] = jnp.where(
            lane == 0, first, jnp.where(lane == 1, second, 0.0)
        )

    def exchange_sums(slots):
        parts = [jnp.transpose(tmp[q * 128 : (q + 1) * 128]) for q in range(4)]
        slots[col] = jnp.concatenate([p[0:1] for p in parts] + [p[1:2] for p in parts], axis=0)
        return [send(slots.at[col], slots.at[col], col_peer(k)) for k in range(1, 16)]

    def spread(line):
        return jnp.transpose(jnp.broadcast_to(line, (128, 128)))

    copies = [
        send(images.at[:, 1:4], halo_lo, strip_up),
        send(images.at[:, 0:3], halo_hi, strip_down),
    ]
    for q in range(4):
        part = slice(q * 128, (q + 1) * 128)
        gg[z, xhi, part] = (cot[part].astype(F32) * lscale[...]).astype(BF16)
    grads = gather_col(gg)
    next(grads)
    win = gather_row(wi, w_in)
    next(win)
    wout = gather_row(wo, w_out)
    next(wout)

    zero_edge = jnp.zeros((2, 10, LEFT, CB), F32)
    pad[:, :, 0:LEFT] = zero_edge
    pad[:, :, LEFT + 64 : 2 * LEFT + 64] = zero_edge
    pad[:, 3:7, LEFT : LEFT + 64] = images[...].astype(F32)
    for copy in copies:
        copy.wait_recv()
    set_halo(halo_lo, halo_hi)

    def after_conv(bh, total):
        conv[pl.ds(pl.multiple_of(bh * 64, 64), 64)] = total
        mean = jnp.sum(total, axis=1, keepdims=True) * (1.0 / CB)
        dev = total - mean
        put_sums(bh, mean, jnp.sum(dev * dev, axis=1, keepdims=True))

    taps_sum(False, after_conv)
    copies = exchange_sums(st1)
    next(grads)
    next(win)
    next(wout)
    for copy in copies:
        copy.wait_recv()
    stats = st1[...]
    means, devs = stats[:, 0:4], stats[:, 4:8]
    mean = jnp.sum(means, axis=0) * (1.0 / 16)
    off = means - mean[None]
    var = (jnp.sum(devs, axis=0) + CB * jnp.sum(off * off, axis=0)) * (1.0 / C)
    inv = lax.rsqrt(var + 1e-06)
    for q in range(4):
        part = slice(q * 128, (q + 1) * 128)
        scale = spread(inv[q : q + 1])
        value = (conv[part] - spread(mean[q : q + 1])) * scale
        istd[part] = scale
        normed[part] = value
        xg[z, xhi, part] = (value * gain[...]).astype(BF16)
    pix = gather_col(xg)
    next(pix)

    def pair(buf, zi):
        return jnp.concatenate([buf[zi, 0], buf[zi, 1]], axis=1)

    def panel(buf, zi):
        xi, yi = zi // NY, zi % NY
        return jnp.concatenate([buf[0, yi, xi], buf[1, yi, xi]], axis=0)

    def product(acc, buf, weight, step, first):
        zi = at_z(step)
        term = jnp.dot(pair(buf, zi), panel(weight, zi), preferred_element_type=F32)
        if first:
            acc[...] = term
        else:
            acc[...] += term

    next(grads)
    next(win)
    next(wout)
    next(pix)
    next(grads)
    next(win)
    next(wout)
    next(pix)
    next(grads)
    next(win)
    next(wout)
    next(pix)
    next(win)
    next(wout)
    next(grads)
    next(pix)
    next(grads)
    product(gh, gg, wo, 0, True)
    for step in (1, -1, 2, -2, 3, -3, 4):
        product(gh, gg, wo, step, False)
    product(hp, xg, wi, 0, True)
    for step in (1, -1, 2, -2):
        product(hp, xg, wi, step, False)
    next(pix)
    next(pix)
    for step in (3, -3, 4):
        product(hp, xg, wi, step, False)

    def activate(i, carry):
        part = pl.ds(pl.multiple_of(i * 64, 64), 64)
        v = hp[part]
        cdf = 0.5 * (1.0 + lax.erf(v * 0.7071067811865476))
        slope = cdf + v * jnp.exp(-0.5 * v * v) * 0.3989422804014327
        hid[part] = (v * cdf).astype(BF16)
        gpre[part] = (gh[part] * slope).astype(BF16)
        return carry

    lax.fori_loop(0, 8, activate, 0)

    def to_channels(dst, act, weight, step):
        zi = at_z(step)
        term = lax.dot_general(
            act[...], panel(weight, zi), CONTRACT_LAST, preferred_element_type=F32
        ).astype(BF16)
        dst[zi, 0] = term[:, 0:CB]
        dst[zi, 1] = term[:, CB : 2 * CB]

    order = (4, -3, 3, -2, 2, -1, 1, 0)
    for step in order:
        to_channels(bk, gpre, wi, step)
    back = scatter_col(bk, bk_m, bk_p, bk_m1, bk_p1, bk_x, bk_xs, bk_xr, gs)
    next(back)

    def weight_grad(dst, buf, act):
        def one(zi, carry):
            xi, yi = zi // NY, zi % NY
            term = lax.dot_general(
                pair(buf, zi), act[...], CONTRACT_FIRST, preferred_element_type=F32
            ).astype(BF16)
            dst[0, yi, xi] = term[0:CB]
            dst[1, yi, xi] = term[CB : 2 * CB]
            return carry

        lax.fori_loop(0, NZ, one, 0)

    weight_grad(g2, gg, hid)
    sum2 = scatter_row(g2, g2_c, g2_m, g2_p, g2_r, g2_r, gp_out)
    next(sum2)
    next(back)
    weight_grad(g1, xg, gpre)
    sum1 = scatter_row(g1, g1_c, g1_m, g1_p, g1_r, g1_r, gp_in)
    next(sum1)
    next(back)
    for step in order:
        to_channels(cb, hid, wo, step)
    next(sum2)
    next(back)
    branch = scatter_col(cb, cb_m, cb_p, cb_m1, cb_p1, cb_x, cb_xs, cb_xr, hp.at[:, 0:CB])
    next(branch)
    next(sum1)
    next(sum2)
    next(back)
    next(back)

    def sums(bh, carry):
        part = pl.ds(pl.multiple_of(bh * 64, 64), 64)
        weighted = gs[part] * gain[...]
        gs[part] = weighted
        put_sums(
            bh,
            jnp.sum(weighted, axis=1, keepdims=True),
            jnp.sum(weighted * normed[part], axis=1, keepdims=True),
        )
        return carry

    lax.fori_loop(0, 8, sums, 0)
    copies = exchange_sums(st2)
    next(branch)
    next(sum1)
    next(sum2)
    for copy in copies:
        copy.wait_recv()
    total = jnp.sum(st2[...], axis=0) * (1.0 / C)
    for q in range(4):
        part = slice(q * 128, (q + 1) * 128)
        value = istd[part] * (
            gs[part] - spread(total[q : q + 1]) - normed[part] * spread(total[4 + q : 5 + q])
        )
        image, line = q // 2, 2 * (q % 2)
        value = value.reshape(2, 64, CB)
        pad[image, 3 + line : 5 + line, LEFT : LEFT + 64] = value
        value = value.astype(BF16)
        if line == 0:
            edge_hi[image, 0:2] = value
            edge_lo[image, 0:1] = value[1:2]
        else:
            edge_hi[image, 2:3] = value[0:1]
            edge_lo[image, 1:3] = value
    copies = [send(edge_lo, ghalo_lo, strip_up), send(edge_hi, ghalo_hi, strip_down)]
    next(branch)
    next(sum1)
    next(sum2)
    for copy in copies:
        copy.wait_recv()
    set_halo(ghalo_lo, ghalo_hi)

    def after_transposed(bh, total):
        part = pl.ds(pl.multiple_of(bh * 64, 64), 64)
        grad_images[bh // 4, bh % 4] = (cot[part].astype(F32) + total).astype(BF16)

    taps_sum(True, after_transposed)

    next(sum1)
    next(branch)
    next(branch)
    next(branch)
    branch_sum = hp.at[:, 0:CB]
    for q in range(8):
        part = slice(q * 64, (q + 1) * 64)
        image, line = q // 4, q % 4
        block_out[image, line] = (
            images[image, line].astype(F32) + lscale[...] * branch_sum[part]
        ).astype(BF16)
    for copy in started:
        copy.wait_send()


def on_device(images, dw_kernel, norm_gain, proj_in, proj_out, layer_scale, cotangent):
    n0 = 512
    n1 = PIX - n0
    a0, a1 = max(n0, 16), max(n1, 16)
    strip = images.shape
    vmem = pltpu.VMEM
    col_blocks = vmem((NZ, 2, PIX, CB), BF16)
    row_blocks = vmem((2, NY, 2, CB, HB), BF16)
    scratch = (
        [vmem((2, 10, 64 + 2 * LEFT, CB), F32)]
        + [vmem((2, 3, 64, CB), BF16)] * 6
        + [vmem((PIX, CB), F32)] * 4
        + [vmem((16, 8, CB), F32)] * 2
        + [col_blocks] * 2
        + [row_blocks] * 2
        + [vmem((PIX, HB), F32)] * 2
        + [vmem((PIX, HB), BF16)] * 2
        + [col_blocks] * 2
        + [vmem((4, 2, a0, CB), BF16)] * 4
        + [vmem((4, a1, CB), BF16)] * 4
        + [vmem((NZ, a1, CB), BF16)] * 2
        + [vmem((a0, CB), BF16)] * 4
        + [vmem((PIX, CB), F32)]
        + [row_blocks] * 2
        + [vmem((NY, 2, CB, HB), BF16)] * 2
        + [vmem((2, 2, CB, HB), BF16)] * 4
        + [vmem((2, CB, HB), BF16)] * 2
        + [pltpu.SemaphoreType.DMA((N_SEMS,))] * 2
    )
    block = pl.BlockSpec(memory_space=pltpu.VMEM)
    return pl.pallas_call(
        functools.partial(kernel, n0),
        out_shape=(
            jax.ShapeDtypeStruct(strip, BF16),
            jax.ShapeDtypeStruct(strip, BF16),
            jax.ShapeDtypeStruct(proj_in.shape, BF16),
            jax.ShapeDtypeStruct(proj_out.shape, BF16),
        ),
        in_specs=[block] * 7,
        out_specs=(block,) * 4,
        scratch_shapes=scratch,
        compiler_params=pltpu.CompilerParams(
            collective_id=0, has_side_effects=True, vmem_limit_bytes=56 << 20
        ),
    )(
        images,
        dw_kernel,
        norm_gain.reshape(1, CB),
        proj_in,
        proj_out,
        layer_scale.reshape(1, CB),
        cotangent.reshape(PIX, CB),
    )


def solution(mesh):
    placed = (
        P(None, "row", None, "col"),
        P(None, None, "col"),
        P("col"),
        P("row", "col"),
        P("row", "col"),
        P("col"),
        P(None, "row", None, "col"),
    )
    return jax.shard_map(
        on_device,
        mesh=mesh,
        in_specs=placed,
        out_specs=(
            P(None, "row", None, "col"),
            P(None, "row", None, "col"),
            P("row", "col"),
            P("row", "col"),
        ),
        check_vma=False,
    )
```

time: 876 us -> 135 us (0.15)
  waiting for transfers between devices: 681 us -> 0 us
  Pallas kernels: 0 us -> 130 us
  blocking collectives: 120 us -> 0 us
  matrix products: 20.5 us -> 0 us
  starting transfers between devices: 15.8 us -> 0 us
  between operations: 14.3 us -> 0.65 us
  local copies, waits for them, and re-layouts: 14.9 us -> 4.16 us
    unnamed x10 -> x0, waiting for transfers between devices: 404 us -> none
    all_gather x4 -> x0, waiting for transfers between devices: 193 us -> none  [the longest x1 83.9 us: on_device(): full_grad = lax.all_gather(grad_branch, 'col', axis=1, tiled=True)]
    pallas_call x0 -> x1, Pallas kernels: none -> 130 us  [on_device(): pl.pallas_call(functools.partial(kernel, n0), out_shape=(jax.ShapeDtypeSt...]
    psum x3 -> x0, blocking collectives: 120 us -> none  [the longest x1 44 us: on_device(): row_mean = lax.psum(jnp.sum(conv_out, axis=1), 'col') / C]
    reduce_scatter x2 -> x0, waiting for transfers between devices: 81.5 us -> none  [the longest x1 67.6 us: on_device(): lax.psum_scatter(lax.dot_general(full_grad, hidden, contract_first, prefe...]
    dot_general x6 -> x0, matrix products: 20.5 us -> none  [the longest x1 6.52 us: on_device(): hidden_pre = jnp.dot(full_in, in_panel, preferred_element_type=jnp.float32)]
    ppermute x4 -> x0, starting transfers between devices: 15.3 us -> none  [the longest x2 11.5 us: with_halo(): lax.ppermute(lax.slice_in_dim(block, 0, width, axis=dim), axis, backward)]
  transfers between devices with their start and end apart: 12 -> 0, of which waited for: 9 -> 0; matrix products, arithmetic and copies ran while one was open for 3% -> 0% of each run, Pallas kernels for 0% -> 0%
where the time goes in v1:
time: 135 us; the launch traced here: 134 us
  Pallas kernels  130 us (96%)
  local copies, waits for them, and re-layouts  4.16 us (3%)
    pallas_call x1, Pallas kernels, on_device(): pl.pallas_call(functools.partial(kernel, n0), out_shape=(jax.ShapeDtypeSt...  130 us
    unnamed x10, local copies, waits for them, and re-layouts  4.16 us

profile of v1, /device:TPU:2, one launch (start us, length us, event | category | flops | bytes accessed | tf_op | source)
XLA Modules:
  0.0 134.4 jit_solution(5260008810792387299)
XLA Ops:
  0.6 129.6 %shard_map.102 = (bf16[2,4,64,128]{3,2,1,0:T(8,128)(2,1)}, bf16[2,4,64,128]{3,2,1,0:T(8,128)(2,1)}, bf16[128,512]{1,0:T(8,128)(2,1)}, bf16[128,512]{1,0:T(8,128)(2,1)}) custom-call(bf16[2,4,64,128]{3,2,1,0:T(8,128)(2,1)} %images.1, f32[7,7,128]{2,1,0:T(8,128)} %dwk.1, f32[1,128]{1,0:T(1,128)} %bitcast.4, bf16[128,512]{1,0:T(8,128)(2,1)} %w_in.1, ...), custom_call_target="tpu_custom_call" | custom-call | tf_op jit(solution)/shard_map/pallas_call | solution.py:590
  130.2 0.0 copy-start.2
  130.2 1.6 %copy.15 = bf16[2,4,64,128]{3,2,1,0:T(8,128)(2,1)} copy(bf16[2,4,64,128]{3,2,1,0:T(8,128)(2,1)} %get-tuple-element.8) | data formatting | bytes 262144
  131.8 0.0 copy-done.2
  131.8 0.0 copy-start.1
  131.8 0.7 copy.16
  132.5 0.3 copy-done.1
  132.8 0.0 copy-start
  132.8 0.7 copy.17
  133.5 0.3 copy-done
  133.7 0.7 copy.18
Async XLA Ops:
  130.2 1.6 %copy-start.2 = (bf16[2,4,64,128]{3,2,1,0:T(8,128)(2,1)S(1)}, bf16[2,4,64,128]{3,2,1,0:T(8,128)(2,1)}, u32[]{:S(2)}) copy-start(bf16[2,4,64,128]{3,2,1,0:T(8,128)(2,1)} %get-tuple-element.9) | copy-start | bytes 393220
  131.8 1.0 copy-start.1
  132.8 1.0 copy-start

commit v2 on v1

--- a/solution.py
+++ b/solution.py
@@ -28,7 +28,7 @@
     block_out, grad_images, gp_in, gp_out,
     pad, halo_lo, halo_hi, ghalo_lo, ghalo_hi, edge_lo, edge_hi,
     conv, normed, istd, tmp, st1, st2,
-    xg, gg, wi, wo, hp, gh, hid, gpre,
+    cols, xg, xs, gg, wi, wo, hp, gh, hid, gpre,
     cb, bk, cb_m, cb_p, bk_m, bk_p, cb_m1, cb_p1, bk_m1, bk_p1,
     cb_x, bk_x, cb_xs, bk_xs, cb_xr, bk_xr, gs,
     g1, g2, g1_c, g2_c, g1_m, g1_p, g2_m, g2_p, g1_r, g2_r,
@@ -70,8 +70,18 @@
         started.append(copy)
         return copy
 
+    zero_edge = jnp.zeros((2, 10, LEFT, CB), F32)
+    pad[:, :, 0:LEFT] = zero_edge
+    pad[:, :, LEFT + 64 : 2 * LEFT + 64] = zero_edge
+    pad[:, 3:7, LEFT : LEFT + 64] = images[...].astype(F32)
+    for q in range(4):
+        part = slice(q * 128, (q + 1) * 128)
+        gg[z, xhi, part] = (cot[part].astype(F32) * lscale[...]).astype(BF16)
+    wi[core, y, xlo] = w_in[...]
+    wo[core, y, xlo] = w_out[...]
+
     barrier = pltpu.get_barrier_semaphore()
-    peers = [strip_up, strip_down, y_up, y_down, x_near] + [col_peer(k) for k in range(1, 16)]
+    peers = [strip_up, strip_down, y_up, y_down, x_near, x_far, z_up, z_down]
     for peer in peers:
         pl.semaphore_signal(barrier, inc=1, device_id=peer, device_id_type=MESH)
     pl.semaphore_wait(barrier, len(peers))
@@ -100,41 +110,52 @@
     def gather_col(buf):
         def rows(zi, half, first, count):
             return buf.at[zi, half, pl.ds(first, count)]
-        waits = {k: [] for k in range(5)}
+
+        far = {k: [] for k in range(5)}
         rings = []
         if n0:
-            far = send(rows(z, xhi, 0, n0), rows(z, xhi, 0, n0), x_far)
-            ring = ring_gather(buf, xhi, 0, n0)
+            near = send(rows(z, xhi, 0, n0), rows(z, xhi, 0, n0), x_far)
+            rings.append(ring_gather(buf, xhi, 0, n0))
+        if n1:
+            rings.append(ring_gather(buf, xhi, n0, n1))
+        for ring in rings:
             next(ring)
-            rings.append(ring)
         if n1:
-            ring1 = ring_gather(buf, xhi, n0, n1)
-            next(ring1)
-            waits[0].append(send(rows(z, xhi, n0, n1), rows(z, xhi, n0, n1), x_far))
-        yield
-        if n0:
-            far.wait_recv()
-            ring = ring_gather(buf, 1 - xhi, 0, n0)
-            next(ring)
-            rings.append(ring)
-        yield
-        for k in (1, 2, 3, 4):
-            if n1:
-                next(ring1)
-                for step in sorted({-k, k} if k < 4 else {4}):
-                    part = rows(at_z(step), xhi, n0, n1)
-                    waits[k].append(send(part, part, x_far))
-            for ring in rings:
-                next(ring)
-            if k == 1:
-                for copy in waits[0]:
-                    copy.wait_recv()
-            if k > 1:
-                for copy in waits[k - 1]:
+            far[0].append(send(rows(z, xhi, n0, n1), rows(z, xhi, n0, n1), x_far))
+        yield
+        late = ring_gather(buf, 1 - xhi, 0, n0)
+        for k in (1, 2, 3, 4, 5):
+            if k < 5:
+                for ring in rings:
+                    next(ring)
+                if n1:
+                    for step in sorted({-k, k} if k < 4 else {4}):
+                        part = rows(at_z(step), xhi, n0, n1)
+                        far[k].append(send(part, part, x_far))
+            if n0:
+                if k == 1:
+                    near.wait_recv()
+                next(late)
+            for i in {1: (), 2: (0,), 3: (1,), 4: (2,), 5: (3, 4)}[k]:
+                for copy in far[i]:
                     copy.wait_recv()
             yield
-        for copy in waits[4]:
-            copy.wait_recv()
+
+    def gather_stats(slots):
+        near = send(slots.at[0, 0], slots.at[0, 1], x_far)
+        yield
+        near.wait_recv()
+        up = send(slots.at[0], slots.at[NZ - 1], z_up)
+        down = send(slots.at[0], slots.at[1], z_down)
+        yield
+        for k in (1, 2, 3):
+            up.wait_recv()
+            up = send(slots.at[NZ - k], slots.at[NZ - k - 1], z_up)
+            down.wait_recv()
+            if k < 3:
+                down = send(slots.at[k], slots.at[k + 1], z_down)
+            yield
+        up.wait_recv()
         yield
 
     def gather_row(buf, own):
@@ -145,7 +166,6 @@
         def share(yi, xi):
             waits.append(send(block(core, yi, xi), block(core, yi, xi), sibling))
 
-        buf[core, y, xlo] = own[...]
         near = send(own, block(core, y, xlo), x_near)
         up, down = {}, {}
         up[0] = send(own, block(core, y, xlo), y_up)
@@ -336,9 +356,12 @@
             lane == 0, first, jnp.where(lane == 1, second, 0.0)
         )
 
+    def packed_sums():
+        parts = [jnp.transpose(tmp[q * 128 : (q + 1) * 128]) for q in range(4)]
+        return jnp.concatenate([p[0:1] for p in parts] + [p[1:2] for p in parts], axis=0)
+
     def exchange_sums(slots):
-        parts = [jnp.transpose(tmp[q * 128 : (q + 1) * 128]) for q in range(4)]
-        slots[col] = jnp.concatenate([p[0:1] for p in parts] + [p[1:2] for p in parts], axis=0)
+        slots[col] = packed_sums()
         return [send(slots.at[col], slots.at[col], col_peer(k)) for k in range(1, 16)]
 
     def spread(line):
@@ -348,9 +371,6 @@
         send(images.at[:, 1:4], halo_lo, strip_up),
         send(images.at[:, 0:3], halo_hi, strip_down),
     ]
-    for q in range(4):
-        part = slice(q * 128, (q + 1) * 128)
-        gg[z, xhi, part] = (cot[part].astype(F32) * lscale[...]).astype(BF16)
     grads = gather_col(gg)
     next(grads)
     win = gather_row(wi, w_in)
@@ -358,42 +378,25 @@
     wout = gather_row(wo, w_out)
     next(wout)
 
-    zero_edge = jnp.zeros((2, 10, LEFT, CB), F32)
-    pad[:, :, 0:LEFT] = zero_edge
-    pad[:, :, LEFT + 64 : 2 * LEFT + 64] = zero_edge
-    pad[:, 3:7, LEFT : LEFT + 64] = images[...].astype(F32)
     for copy in copies:
         copy.wait_recv()
     set_halo(halo_lo, halo_hi)
 
     def after_conv(bh, total):
-        conv[pl.ds(pl.multiple_of(bh * 64, 64), 64)] = total
+        part = pl.ds(pl.multiple_of(bh * 64, 64), 64)
+        conv[part] = total
         mean = jnp.sum(total, axis=1, keepdims=True) * (1.0 / CB)
         dev = total - mean
+        xg[z, xhi, part] = dev.astype(BF16)
         put_sums(bh, mean, jnp.sum(dev * dev, axis=1, keepdims=True))
 
     taps_sum(False, after_conv)
-    copies = exchange_sums(st1)
-    next(grads)
-    next(win)
-    next(wout)
-    for copy in copies:
-        copy.wait_recv()
-    stats = st1[...]
-    means, devs = stats[:, 0:4], stats[:, 4:8]
-    mean = jnp.sum(means, axis=0) * (1.0 / 16)
-    off = means - mean[None]
-    var = (jnp.sum(devs, axis=0) + CB * jnp.sum(off * off, axis=0)) * (1.0 / C)
-    inv = lax.rsqrt(var + 1e-06)
-    for q in range(4):
-        part = slice(q * 128, (q + 1) * 128)
-        scale = spread(inv[q : q + 1])
-        value = (conv[part] - spread(mean[q : q + 1])) * scale
-        istd[part] = scale
-        normed[part] = value
-        xg[z, xhi, part] = (value * gain[...]).astype(BF16)
     pix = gather_col(xg)
     next(pix)
+    st1[0, 0, 0:8] = packed_sums()
+    st1[0, 0, 8:16] = jnp.broadcast_to(gain[...], (8, CB))
+    stats = gather_stats(st1)
+    next(stats)
 
     def pair(buf, zi):
         return jnp.concatenate([buf[zi, 0], buf[zi, 1]], axis=1)
@@ -410,33 +413,67 @@
         else:
             acc[...] += term
 
+    def normalise(step):
+        for other in (0, 1):
+            slot = (step % NZ, other)
+            half = xhi if other == 0 else 1 - xhi
+            place = slot[0] * 2 + other
+            scale = st1[slot[0], other, 8:9]
+            for q in range(4):
+                part = slice(q * 128, (q + 1) * 128)
+                dev = xg[at_z(step), half, part].astype(F32)
+                value = (dev + cols[q, :, place : place + 1]) * istd[part] * scale
+                xs[at_z(step), half, part] = value.astype(BF16)
+
     next(grads)
     next(win)
     next(wout)
     next(pix)
+    next(stats)
     next(grads)
     next(win)
     next(wout)
+    next(stats)
     next(pix)
     next(grads)
     next(win)
     next(wout)
+    next(stats)
     next(pix)
+    next(grads)
     next(win)
     next(wout)
-    next(grads)
+    next(stats)
     next(pix)
     next(grads)
+    next(win)
+    next(wout)
+    next(stats)
+    every = st1[...]
+    means, devs = every[:, :, 0:4], every[:, :, 4:8]
+    mean = jnp.sum(means, axis=(0, 1)) * (1.0 / 16)
+    shift = means - mean[None, None]
+    var = (jnp.sum(devs, axis=(0, 1)) + CB * jnp.sum(shift * shift, axis=(0, 1))) * (1.0 / C)
+    inv = lax.rsqrt(var + 1e-06)
+    for q in range(4):
+        part = slice(q * 128, (q + 1) * 128)
+        lines = [shift[o, i, q : q + 1] for o in range(NZ) for i in range(2)]
+        lines += [inv[q : q + 1], mean[q : q + 1], jnp.zeros((110, 128), F32)]
+        turned = jnp.transpose(jnp.concatenate(lines, axis=0))
+        cols[q] = turned
+        scale = jnp.broadcast_to(turned[:, 16:17], (128, CB))
+        istd[part] = scale
+        normed[part] = (conv[part] - turned[:, 17:18]) * scale
     product(gh, gg, wo, 0, True)
     for step in (1, -1, 2, -2, 3, -3, 4):
         product(gh, gg, wo, step, False)
-    product(hp, xg, wi, 0, True)
-    for step in (1, -1, 2, -2):
-        product(hp, xg, wi, step, False)
-    next(pix)
+    for step in (0, 1, -1, 2, -2):
+        normalise(step)
+        product(hp, xs, wi, step, step == 0)
     next(pix)
     for step in (3, -3, 4):
-        product(hp, xg, wi, step, False)
+        normalise(step)
+        product(hp, xs, wi, step, False)
 
     def activate(i, carry):
         part = pl.ds(pl.multiple_of(i * 64, 64), 64)
@@ -479,7 +516,7 @@
     sum2 = scatter_row(g2, g2_c, g2_m, g2_p, g2_r, g2_r, gp_out)
     next(sum2)
     next(back)
-    weight_grad(g1, xg, gpre)
+    weight_grad(g1, xs, gpre)
     sum1 = scatter_row(g1, g1_c, g1_m, g1_p, g1_r, g1_r, gp_in)
     next(sum1)
     next(back)
@@ -558,7 +595,7 @@
 
 
 def on_device(images, dw_kernel, norm_gain, proj_in, proj_out, layer_scale, cotangent):
-    n0 = 512
+    n0 = 256
     n1 = PIX - n0
     a0, a1 = max(n0, 16), max(n1, 16)
     strip = images.shape
@@ -569,8 +606,8 @@
         [vmem((2, 10, 64 + 2 * LEFT, CB), F32)]
         + [vmem((2, 3, 64, CB), BF16)] * 6
         + [vmem((PIX, CB), F32)] * 4
-        + [vmem((16, 8, CB), F32)] * 2
-        + [col_blocks] * 2
+        + [vmem((NZ, 2, 16, CB), F32), vmem((16, 8, CB), F32), vmem((4, 128, 128), F32)]
+        + [col_blocks] * 3
         + [row_blocks] * 2
         + [vmem((PIX, HB), F32)] * 2
         + [vmem((PIX, HB), BF16)] * 2

time: 135 us -> 116 us (0.86)
  Pallas kernels: 130 us -> 111 us
    pallas_call x1, Pallas kernels: 130 us -> 111 us  [on_device(): pl.pallas_call(functools.partial(kernel, n0), out_shape=(jax.ShapeDtypeSt...]
where the time goes in v2:
time: 116 us
  Pallas kernels  111 us (96%)
  local copies, waits for them, and re-layouts  4.16 us (4%)
    pallas_call x1, Pallas kernels, on_device(): pl.pallas_call(functools.partial(kernel, n0), out_shape=(jax.ShapeDtypeSt...  111 us
    unnamed x10, local copies, waits for them, and re-layouts  4.16 us

profile of v2, /device:TPU:2, one launch (start us, length us, event | category | flops | bytes accessed | tf_op | source)
XLA Modules:
  0.0 116.1 jit_solution(209215238693015345)
XLA Ops:
  0.6 111.3 %shard_map.102 = (bf16[2,4,64,128]{3,2,1,0:T(8,128)(2,1)}, bf16[2,4,64,128]{3,2,1,0:T(8,128)(2,1)}, bf16[128,512]{1,0:T(8,128)(2,1)}, bf16[128,512]{1,0:T(8,128)(2,1)}) custom-call(bf16[2,4,64,128]{3,2,1,0:T(8,128)(2,1)} %images.1, f32[7,7,128]{2,1,0:T(8,128)} %dwk.1, f32[1,128]{1,0:T(1,128)} %bitcast.4, bf16[128,512]{1,0:T(8,128)(2,1)} %w_in.1, ...), custom_call_target="tpu_custom_call" | custom-call | tf_op jit(solution)/shard_map/pallas_call | solution.py:627
  111.9 0.0 copy-start.2
  112.0 1.6 %copy.15 = bf16[2,4,64,128]{3,2,1,0:T(8,128)(2,1)} copy(bf16[2,4,64,128]{3,2,1,0:T(8,128)(2,1)} %get-tuple-element.8) | data formatting | bytes 262144
  113.6 0.0 copy-done.2
  113.6 0.0 copy-start.1
  113.6 0.7 copy.16
  114.2 0.3 copy-done.1
  114.5 0.0 copy-start
  114.5 0.7 copy.17
  115.2 0.3 copy-done
  115.5 0.7 copy.18
Async XLA Ops:
  111.9 1.6 %copy-start.2 = (bf16[2,4,64,128]{3,2,1,0:T(8,128)(2,1)S(1)}, bf16[2,4,64,128]{3,2,1,0:T(8,128)(2,1)}, u32[]{:S(2)}) copy-start(bf16[2,4,64,128]{3,2,1,0:T(8,128)(2,1)} %get-tuple-element.9) | copy-start | bytes 393220
  113.6 1.0 copy-start.1
  114.5 1.0 copy-start

commit v3 on v2

v3 whole, which is shorter than its diff:
```python
import functools

import jax
import jax.numpy as jnp
from jax import lax
from jax.experimental import pallas as pl
from jax.experimental.pallas import tpu as pltpu
from jax.sharding import PartitionSpec as P

MESH = pl.DeviceIdType.MESH
F32, BF16 = jnp.float32, jnp.bfloat16
C = 2048
KS = 7
NZ, NY = 8, 4
CB = 128
HB = 512
PIX = 512
LEFT = 8
TAP0 = LEFT - KS // 2
N_SEND, N_RECV = 21, 165
GATHER_ORDER = "gGWwxXSgGWwSxXgGWwSxXgGWwSxXgWwSx"
BACK_ORDER = "mMBknNbBMcCbBNcCbBMcCbBNB"
HALO_ORDER = "McCN"
LAST_ORDER = "MNCC"
CONTRACT_LAST = (((1,), (1,)), ((), ()))
CONTRACT_FIRST = (((0,), (0,)), ((), ()))


def kernel(
    n0,
    images, dwk, gain, w_in, w_out, lscale, cot,
    block_out, grad_images, gp_in, gp_out,
    pad, halo_lo, halo_hi, ghalo_lo, ghalo_hi, edge_lo, edge_hi,
    conv, normed, istd, tmp, st1, st2,
    cols, xg, xs, gg, wi, wo, hp, gh, hid, gpre,
    gw, cb, bk, cb_m, cb_p, bk_m, bk_p, cb_mo, cb_po, bk_mo, bk_po,
    cb_x, bk_x, cb_xs, bk_xs, cb_xr, bk_xr, gs,
    g1, g2, g1_c, g2_c, g1_m, g1_p, g2_m, g2_p, g1_r, g2_r,
    send_sem, recv_sem,
):
    n1 = PIX - n0
    row, col = lax.axis_index("row"), lax.axis_index("col")
    xlo, y, core = row // 8, (row // 2) % NY, row % 2
    z, xhi = col // 2, col % 2

    def at_z(step):
        return (z + step + NZ) % NZ

    def at_y(step):
        return (y + step + NY) % NY

    z_up = {"row": row, "col": at_z(1) * 2 + xhi}
    z_down = {"row": row, "col": at_z(-1) * 2 + xhi}
    x_far = {"row": row, "col": z * 2 + (1 - xhi)}
    y_up = {"row": xlo * 8 + at_y(1) * 2 + core, "col": col}
    y_down = {"row": xlo * 8 + at_y(-1) * 2 + core, "col": col}
    x_near = {"row": (1 - xlo) * 8 + y * 2 + core, "col": col}
    sibling = {"row": xlo * 8 + y * 2 + (1 - core), "col": col}
    strip_up = {"row": (row + 1) % 16, "col": col}
    strip_down = {"row": (row + 15) % 16, "col": col}

    def col_peer(step):
        return {"row": row, "col": (col + step) % 16}

    counts = {"recv": 0, "send": 0}

    def take(kind):
        counts[kind] += 1
        return counts[kind] - 1

    sends = []

    def group(whole):
        sends.append((take("send"), whole))
        return sends[-1][0]

    def send(src, dst, where, sem=None, recv=None):
        if sem is None:
            sem = group(src)
        copy = pltpu.make_async_remote_copy(
            src_ref=src, dst_ref=dst, send_sem=send_sem.at[sem],
            recv_sem=recv_sem.at[take("recv") if recv is None else recv],
            device_id=where, device_id_type=MESH,
        )
        copy.start()
        return copy

    def blocks15():
        return group(xg.at[0:15])

    zero_edge = jnp.zeros((2, 10, LEFT, CB), F32)
    pad[:, :, 0:LEFT] = zero_edge
    pad[:, :, LEFT + 64 : 2 * LEFT + 64] = zero_edge
    pad[:, 3:7, LEFT : LEFT + 64] = images[...].astype(F32)
    for q in range(4):
        part = slice(q * 128, (q + 1) * 128)
        gg[col, part] = (cot[part].astype(F32) * lscale[...]).astype(BF16)
    wi[core, y, xlo] = w_in[...]
    wo[core, y, xlo] = w_out[...]

    barrier = pltpu.get_barrier_semaphore()
    peers = [strip_up, strip_down, y_up, y_down, x_near, x_far, z_up, z_down]
    for peer in peers:
        pl.semaphore_signal(barrier, inc=1, device_id=peer, device_id_type=MESH)
    pl.semaphore_wait(barrier, len(peers))

    def ring_gather(buf, half, count, sem):
        def block(zi, lo=0, n=count):
            return buf.at[zi * 2 + half, pl.ds(lo, n)]

        up = send(block(z), block(z), z_up, sem)
        down = send(block(z), block(z), z_down, sem)
        yield
        for k in (1, 2, 3):
            if k < 3:
                up.wait_recv()
                up = send(block(at_z(-k)), block(at_z(-k)), z_up, sem)
                down.wait_recv()
                down = send(block(at_z(k)), block(at_z(k)), z_down, sem)
            else:
                h = count // 2
                up.wait_recv()
                up = send(block(at_z(-3), 0, h), block(at_z(-3), 0, h), z_up, sem)
                down.wait_recv()
                down = send(block(at_z(3), h, h), block(at_z(3), h, h), z_down, sem)
            yield
        up.wait_recv()
        down.wait_recv()
        yield

    def gather_col(buf):
        sem = blocks15()
        far = []

        def rows(zi, half, first, count):
            return buf.at[zi * 2 + half, pl.ds(first, count)]

        def own():
            ring = ring_gather(buf, xhi, PIX, sem)
            near = send(rows(z, xhi, 0, n0), rows(z, xhi, 0, n0), x_far, sem)
            next(ring)
            far.append(send(rows(z, xhi, n0, n1), rows(z, xhi, n0, n1), x_far, sem))
            yield near
            for k in (1, 2, 3, 4):
                next(ring)
                for step in (-k, k) if k < 4 else (4,):
                    part = rows(at_z(step), xhi, n0, n1)
                    far.append(send(part, part, x_far, sem))
                yield

        def other(near):
            near.wait_recv()
            ring = ring_gather(buf, 1 - xhi, n0, sem)
            for k in range(5):
                next(ring)
                yield

        def rest(count):
            for copy in far[:count]:
                copy.wait_recv()
            del far[:count]

        first = own()
        second = other(next(first))
        return first, second, rest

    def gather_stats(slots):
        near = send(slots.at[0, 0], slots.at[0, 1], x_far)
        yield
        near.wait_recv()
        up = send(slots.at[0], slots.at[NZ - 1], z_up)
        down = send(slots.at[0], slots.at[1], z_down)
        yield
        for k in (1, 2, 3):
            up.wait_recv()
            up = send(slots.at[NZ - k], slots.at[NZ - k - 1], z_up)
            down.wait_recv()
            if k < 3:
                down = send(slots.at[k], slots.at[k + 1], z_down)
            yield
        up.wait_recv()
        yield

    def gather_row(buf, own):
        def block(k, yi, xi, lo=0, n=CB):
            return buf.at[k, yi, xi, pl.ds(lo, n)]
        waits = []
        sem = blocks15()

        def share(yi, xi):
            waits.append(send(block(core, yi, xi), block(core, yi, xi), sibling, sem))

        near = send(own, block(core, y, xlo), x_near, sem)
        up, down = {}, {}
        up[0] = send(own, block(core, y, xlo), y_up, sem)
        down[0] = send(own, block(core, y, xlo), y_down, sem)
        waits.append(send(own, block(core, y, xlo), sibling, sem))
        yield
        near.wait_recv()
        other = 1 - xlo
        up[1] = send(block(core, y, other), block(core, y, other), y_up, sem)
        down[1] = send(block(core, y, other), block(core, y, other), y_down, sem)
        share(y, other)
        yield
        h = CB // 2
        for i, xi in enumerate((xlo, other)):
            up[i].wait_recv()
            down[i].wait_recv()
            low, high = block(core, at_y(-1), xi, 0, h), block(core, at_y(1), xi, h, h)
            up[i] = send(low, low, y_up, sem)
            down[i] = send(high, high, y_down, sem)
            share(at_y(-1), xi)
            share(at_y(1), xi)
            yield
        for i, xi in enumerate((xlo, other)):
            up[i].wait_recv()
            down[i].wait_recv()
            share(at_y(2), xi)
        yield
        for copy in waits:
            copy.wait_recv()
        yield

    def add_into(dst, src):
        dst[...] = (dst[...].astype(F32) + src[...].astype(F32)).astype(BF16)

    def ring_scatter(buf, half, count, rm, rp, ready, sem):
        h = count // 2

        def block(zi, lo=0, n=count):
            return buf.at[zi * 2 + half, pl.ds(lo, n)]

        ready(4)
        down = send(block(at_z(-4), 0, h), rm.at[0, pl.ds(0, h)], z_down, sem)
        up = send(block(at_z(4), h, h), rp.at[0, pl.ds(0, h)], z_up, sem)
        yield
        for k in (2, 3, 4):
            dist = 5 - k
            ready(-dist)
            ready(dist)
            down.wait_recv()
            if k == 2:
                add_into(block(at_z(-dist), 0, h), rm.at[0, pl.ds(0, h)])
            else:
                add_into(block(at_z(-dist)), rm.at[k - 2])
            down = send(block(at_z(-dist)), rm.at[k - 1], z_down, sem)
            up.wait_recv()
            if k == 2:
                add_into(block(at_z(dist), h, h), rp.at[0, pl.ds(0, h)])
            else:
                add_into(block(at_z(dist)), rp.at[k - 2])
            up = send(block(at_z(dist)), rp.at[k - 1], z_up, sem)
            yield
        ready(0)
        down.wait_recv()
        up.wait_recv()
        yield

    def scatter_col(buf, rm, rp, rmo, rpo, rx, xs_, xr, total):
        sem = blocks15()
        far = {}

        def offer(step):
            zi = at_z(step)
            far[step % NZ] = send(
                buf.at[zi * 2 + 1 - xhi, pl.ds(n0, n1)], rx.at[zi], x_far, sem
            )

        def ready(step):
            zi = at_z(step)
            far[step % NZ].wait_recv()
            add_into(buf.at[zi * 2 + xhi, pl.ds(n0, n1)], rx.at[zi])

        last = []

        def other():
            half = 1 - xhi
            ring = ring_scatter(buf, half, n0, rmo, rpo, lambda step: None, sem)
            for k in range(4):
                next(ring)
                yield
            next(ring)
            xs_[...] = (
                buf[z * 2 + half, 0:n0].astype(F32) + rmo[3].astype(F32) + rpo[3].astype(F32)
            ).astype(BF16)
            last.append(send(xs_, xr, x_far, sem))
            yield

        def own():
            ring = ring_scatter(buf, xhi, PIX, rm, rp, ready, sem)
            for k in range(5):
                next(ring)
                yield
            last[0].wait_recv()
            both = buf[z * 2 + xhi].astype(F32) + rm[3].astype(F32) + rp[3].astype(F32)
            total[0:n0] = both[0:n0] + xr[...].astype(F32)
            total[n0:PIX] = both[n0:PIX]
            yield

        return offer, other(), own()

    def scatter_row(buf, rc, rm, rp, rx, xs_slot, out):
        h = CB // 2
        shared = {}
        sem = blocks15()
        for step in (2, -1, 1, 0):
            shared[step] = send(buf.at[1 - core, at_y(step)], rc.at[at_y(step)], sibling, sem)
        yield
        shared[2].wait_recv()
        add_into(buf.at[core, at_y(2)], rc.at[at_y(2)])
        down = send(
            buf.at[core, at_y(-2), :, pl.ds(0, h)], rm.at[0, :, pl.ds(0, h)], y_down, sem
        )
        up = send(buf.at[core, at_y(2), :, pl.ds(h, h)], rp.at[0, :, pl.ds(0, h)], y_up, sem)
        for step in (-1, 1, 0):
            shared[step].wait_recv()
            add_into(buf.at[core, at_y(step)], rc.at[at_y(step)])
        yield
        down.wait_recv()
        add_into(buf.at[core, at_y(-1), :, pl.ds(0, h)], rm.at[0, :, pl.ds(0, h)])
        down = send(buf.at[core, at_y(-1)], rm.at[1], y_down, sem)
        up.wait_recv()
        add_into(buf.at[core, at_y(1), :, pl.ds(h, h)], rp.at[0, :, pl.ds(0, h)])
        up = send(buf.at[core, at_y(1)], rp.at[1], y_up, sem)
        yield
        down.wait_recv()
        up.wait_recv()
        theirs = 1 - xlo
        xs_slot[0] = (
            buf[core, y, theirs].astype(F32)
            + rm[1, theirs].astype(F32)
            + rp[1, theirs].astype(F32)
        ).astype(BF16)
        near = send(xs_slot.at[0], rx.at[1], x_near, sem)
        yield
        near.wait_recv()
        out[...] = (
            buf[core, y, xlo].astype(F32)
            + rm[1, xlo].astype(F32)
            + rp[1, xlo].astype(F32)
            + rx[1].astype(F32)
        ).astype(BF16)
        yield

    def taps_sum(flipped, finish):
        def strip_row(bh, carry):
            image, line = bh // 4, bh % 4
            total = jnp.zeros((64, CB), F32)
            for i in range(KS):
                for j in range(KS):
                    tap = dwk[KS - 1 - i, pl.ds(KS - 1 - j, 1)] if flipped else dwk[i, pl.ds(j, 1)]
                    total = total + tap * pad[image, line + i, pl.ds(TAP0 + j, 64)]
            finish(bh, total)
            return carry

        lax.fori_loop(0, 8, strip_row, 0)

    def set_halo(low, high):
        pad[:, 0:3, LEFT : LEFT + 64] = jnp.where(row > 0, low[...].astype(F32), 0.0)
        pad[:, 7:10, LEFT : LEFT + 64] = jnp.where(row < 15, high[...].astype(F32), 0.0)

    lane = lax.broadcasted_iota(jnp.int32, (64, CB), 1)

    def put_sums(bh, first, second):
        tmp[pl.ds(pl.multiple_of(bh * 64, 64), 64)] = jnp.where(
            lane == 0, first, jnp.where(lane == 1, second, 0.0)
        )

    def packed_sums():
        parts = [jnp.transpose(tmp[q * 128 : (q + 1) * 128]) for q in range(4)]
        return jnp.concatenate([p[0:1] for p in parts] + [p[1:2] for p in parts], axis=0)

    def exchange_sums(slots):
        slots[col] = packed_sums()
        sem, recv = group(slots.at[0:15]), take("recv")
        for k in range(1, 16):
            send(slots.at[col], slots.at[col], col_peer(k), sem, recv)
        return pltpu.make_async_remote_copy(
            src_ref=slots.at[0:15], dst_ref=slots.at[0:15], send_sem=send_sem.at[sem],
            recv_sem=recv_sem.at[recv], device_id=col_peer(1), device_id_type=MESH,
        )

    def spread(line):
        return jnp.transpose(jnp.broadcast_to(line, (128, 128)))

    copies = [
        send(images.at[:, 1:4], halo_lo, strip_up),
        send(images.at[:, 0:3], halo_hi, strip_down),
    ]
    grads, grads2, grads_rest = gather_col(gg)
    win = gather_row(wi, w_in)
    next(win)
    wout = gather_row(wo, w_out)
    next(wout)

    for copy in copies:
        copy.wait_recv()
    set_halo(halo_lo, halo_hi)

    def after_conv(bh, total):
        part = pl.ds(pl.multiple_of(bh * 64, 64), 64)
        conv[part] = total
        mean = jnp.sum(total, axis=1, keepdims=True) * (1.0 / CB)
        dev = total - mean
        xg[col, part] = dev.astype(BF16)
        put_sums(bh, mean, jnp.sum(dev * dev, axis=1, keepdims=True))

    taps_sum(False, after_conv)
    pix, pix2, pix_rest = gather_col(xg)
    st1[0, 0, 0:8] = packed_sums()
    st1[0, 0, 8:16] = jnp.broadcast_to(gain[...], (8, CB))
    stats = gather_stats(st1)
    next(stats)

    def pair(buf, zi):
        return jnp.concatenate([buf[zi * 2], buf[zi * 2 + 1]], axis=1)

    def panel(buf, zi):
        xi, yi = zi // NY, zi % NY
        return jnp.concatenate([buf[0, yi, xi], buf[1, yi, xi]], axis=0)

    def product(acc, buf, weight, step, first):
        zi = at_z(step)
        term = jnp.dot(pair(buf, zi), panel(weight, zi), preferred_element_type=F32)
        if first:
            acc[...] = term
        else:
            acc[...] += term

    def normalise(step):
        for other in (0, 1):
            slot = (step % NZ, other)
            half = xhi if other == 0 else 1 - xhi
            place = slot[0] * 2 + other
            scale = st1[slot[0], other, 8:9]
            for q in range(4):
                part = slice(q * 128, (q + 1) * 128)
                dev = xg[at_z(step) * 2 + half, part].astype(F32)
                value = (dev + cols[q, :, place : place + 1]) * istd[part] * scale
                xs[at_z(step) * 2 + half, part] = value.astype(BF16)

    streams = dict(G=grads, g=grads2, X=pix, x=pix2, W=win, w=wout, S=stats)
    for name in GATHER_ORDER:
        next(streams[name])
    every = st1[...]
    means, devs = every[:, :, 0:4], every[:, :, 4:8]
    mean = jnp.sum(means, axis=(0, 1)) * (1.0 / 16)
    shift = means - mean[None, None]
    var = (jnp.sum(devs, axis=(0, 1)) + CB * jnp.sum(shift * shift, axis=(0, 1))) * (1.0 / C)
    inv = lax.rsqrt(var + 1e-06)
    for q in range(4):
        part = slice(q * 128, (q + 1) * 128)
        lines = [shift[o, i, q : q + 1] for o in range(NZ) for i in range(2)]
        lines += [inv[q : q + 1], mean[q : q + 1], jnp.zeros((110, 128), F32)]
        turned = jnp.transpose(jnp.concatenate(lines, axis=0))
        cols[q] = turned
        scale = jnp.broadcast_to(turned[:, 16:17], (128, CB))
        istd[part] = scale
        normed[part] = (conv[part] - turned[:, 17:18]) * scale
    grads_rest(8)
    product(gh, gg, wo, 0, True)
    for step in (1, -1, 2, -2, 3, -3, 4):
        product(gh, gg, wo, step, False)

    def gain_product(step, first):
        mine, theirs = st1[step % NZ, 0, 8:16], st1[step % NZ, 1, 8:16]
        gains = jnp.concatenate(
            [jnp.where(xhi == 0, mine, theirs), jnp.where(xhi == 0, theirs, mine)], axis=1
        )
        high = gains.astype(BF16)
        low = (gains - high.astype(F32)).astype(BF16)
        parts = jnp.concatenate([high, low], axis=0)
        term = jnp.dot(parts, panel(wi, at_z(step)), preferred_element_type=F32)
        term = term[0:8] + term[8:16]
        if first:
            gw[...] = term
        else:
            gw[...] += term

    for step in (0, 1, -1, 2, -2, 3, -3, 4):
        gain_product(step, step == 0)
    for count, steps in ((1, (0,)), (2, (1, -1)), (2, (2, -2)), (3, (3, -3, 4))):
        pix_rest(count)
        for step in steps:
            normalise(step)
            product(hp, xs, wi, step, step == 0)

    def activate(i, carry):
        part = pl.ds(pl.multiple_of(i * 64, 64), 64)
        v = hp[part]
        cdf = 0.5 * (1.0 + lax.erf(v * 0.7071067811865476))
        slope = cdf + v * jnp.exp(-0.5 * v * v) * 0.3989422804014327
        hid[part] = (v * cdf).astype(BF16)
        grad = (gh[part] * slope).astype(BF16)
        gpre[part] = grad
        grad = grad.astype(F32)
        put_sums(
            i,
            jnp.sum(grad * gw[0:1], axis=1, keepdims=True),
            jnp.sum(grad * v, axis=1, keepdims=True),
        )
        return carry

    lax.fori_loop(0, 8, activate, 0)

    def to_channels(dst, act, weight, step):
        zi = at_z(step)
        term = lax.dot_general(
            act[...], panel(weight, zi), CONTRACT_LAST, preferred_element_type=F32
        ).astype(BF16)
        dst[zi * 2] = term[:, 0:CB]
        dst[zi * 2 + 1] = term[:, CB : 2 * CB]

    def weight_grad(dst, buf, act):
        def one(zi, carry):
            xi, yi = zi // NY, zi % NY
            term = lax.dot_general(
                pair(buf, zi), act[...], CONTRACT_FIRST, preferred_element_type=F32
            ).astype(BF16)
            dst[0, yi, xi] = term[0:CB]
            dst[1, yi, xi] = term[CB : 2 * CB]
            return carry

        lax.fori_loop(0, NZ, one, 0)

    steps = (4, -3, 3, -2, 2, -1, 1, 0)
    offer_b, back2, back = scatter_col(bk, bk_m, bk_p, bk_mo, bk_po, bk_x, bk_xs, bk_xr, gs)
    offer_c, branch2, branch = scatter_col(
        cb, cb_m, cb_p, cb_mo, cb_po, cb_x, cb_xs, cb_xr, hp.at[:, 0:CB]
    )
    for step in steps:
        to_channels(bk, gpre, wi, step)
        offer_b(step)
        if step == 4:
            next(back2)
    totals = exchange_sums(st2)
    streams = dict(
        b=back2, B=back, c=branch2, C=branch,
        M=scatter_row(g2, g2_c, g2_m, g2_p, g2_r, g2_r, gp_out),
        N=scatter_row(g1, g1_c, g1_m, g1_p, g1_r, g1_r, gp_in),
    )

    def contrib():
        for step in steps:
            to_channels(cb, hid, wo, step)
            offer_c(step)
            if step == 4:
                next(branch2)

    def run(order):
        for name in order:
            if name == "k":
                contrib()
            elif name == "m":
                weight_grad(g2, gg, hid)
            elif name == "n":
                weight_grad(g1, xs, gpre)
            else:
                next(streams[name])

    run(BACK_ORDER)

    totals.wait_recv()
    total = jnp.sum(st2[...], axis=0) * (1.0 / C)
    for q in range(4):
        part = slice(q * 128, (q + 1) * 128)
        value = istd[part] * (
            gs[part] * gain[...] - spread(total[q : q + 1]) - normed[part] * spread(total[4 + q : 5 + q])
        )
        image, line = q // 2, 2 * (q % 2)
        value = value.reshape(2, 64, CB)
        pad[image, 3 + line : 5 + line, LEFT : LEFT + 64] = value
        value = value.astype(BF16)
        if line == 0:
            edge_hi[image, 0:2] = value
            edge_lo[image, 0:1] = value[1:2]
        else:
            edge_hi[image, 2:3] = value[0:1]
            edge_lo[image, 1:3] = value
    copies = [send(edge_lo, ghalo_lo, strip_up), send(edge_hi, ghalo_hi, strip_down)]
    run(HALO_ORDER)
    for copy in copies:
        copy.wait_recv()
    set_halo(ghalo_lo, ghalo_hi)

    def after_transposed(bh, total):
        part = pl.ds(pl.multiple_of(bh * 64, 64), 64)
        grad_images[bh // 4, bh % 4] = (cot[part].astype(F32) + total).astype(BF16)

    taps_sum(True, after_transposed)

    run(LAST_ORDER)
    branch_sum = hp.at[:, 0:CB]
    for q in range(8):
        part = slice(q * 64, (q + 1) * 64)
        image, line = q // 4, q % 4
        block_out[image, line] = (
            images[image, line].astype(F32) + lscale[...] * branch_sum[part]
        ).astype(BF16)
    for sem, whole in sends:
        pltpu.make_async_remote_copy(
            src_ref=whole, dst_ref=whole, send_sem=send_sem.at[sem], recv_sem=recv_sem.at[0],
            device_id=z_up, device_id_type=MESH,
        ).wait_send()
    assert counts["recv"] <= N_RECV and counts["send"] <= N_SEND, counts
    for name, stream in streams.items():
        assert next(stream, None) is None, name


def on_device(images, dw_kernel, norm_gain, proj_in, proj_out, layer_scale, cotangent):
    n0 = 256
    n1 = PIX - n0
    strip = images.shape
    vmem = pltpu.VMEM
    col_blocks = vmem((2 * NZ, PIX, CB), BF16)
    row_blocks = vmem((2, NY, 2, CB, HB), BF16)
    scratch = (
        [vmem((2, 10, 64 + 2 * LEFT, CB), F32)]
        + [vmem((2, 3, 64, CB), BF16)] * 6
        + [vmem((PIX, CB), F32)] * 4
        + [vmem((NZ, 2, 16, CB), F32), vmem((16, 8, CB), F32), vmem((4, 128, 128), F32)]
        + [col_blocks] * 3
        + [row_blocks] * 2
        + [vmem((PIX, HB), F32)] * 2
        + [vmem((PIX, HB), BF16)] * 2
        + [vmem((8, HB), F32)]
        + [col_blocks] * 2
        + [vmem((4, PIX, CB), BF16)] * 4
        + [vmem((4, n0, CB), BF16)] * 4
        + [vmem((NZ, n1, CB), BF16)] * 2
        + [vmem((n0, CB), BF16)] * 4
        + [vmem((PIX, CB), F32)]
        + [row_blocks] * 2
        + [vmem((NY, 2, CB, HB), BF16)] * 2
        + [vmem((2, 2, CB, HB), BF16)] * 4
        + [vmem((2, CB, HB), BF16)] * 2
        + [pltpu.SemaphoreType.DMA((N_SEND,)), pltpu.SemaphoreType.DMA((N_RECV,))]
    )
    block = pl.BlockSpec(memory_space=pltpu.VMEM)
    return pl.pallas_call(
        functools.partial(kernel, n0),
        out_shape=(
            jax.ShapeDtypeStruct(strip, BF16),
            jax.ShapeDtypeStruct(strip, BF16),
            jax.ShapeDtypeStruct(proj_in.shape, BF16),
            jax.ShapeDtypeStruct(proj_out.shape, BF16),
        ),
        in_specs=[block] * 7,
        out_specs=(block,) * 4,
        scratch_shapes=scratch,
        compiler_params=pltpu.CompilerParams(
            collective_id=0, has_side_effects=True, vmem_limit_bytes=56 << 20
        ),
    )(
        images,
        dw_kernel,
        norm_gain.reshape(1, CB),
        proj_in,
        proj_out,
        layer_scale.reshape(1, CB),
        cotangent.reshape(PIX, CB),
    )


def solution(mesh):
    placed = (
        P(None, "row", None, "col"),
        P(None, None, "col"),
        P("col"),
        P("row", "col"),
        P("row", "col"),
        P("col"),
        P(None, "row", None, "col"),
    )
    return jax.shard_map(
        on_device,
        mesh=mesh,
        in_specs=placed,
        out_specs=(
            P(None, "row", None, "col"),
            P(None, "row", None, "col"),
            P("row", "col"),
            P("row", "col"),
        ),
        check_vma=False,
    )
```

time: 116 us -> 106 us (0.914)
  Pallas kernels: 111 us -> 101 us
    pallas_call x1, Pallas kernels: 111 us -> 101 us  [on_device(): pl.pallas_call(functools.partial(kernel, n0), out_shape=(jax.ShapeDtypeSt...]
where the time goes in v3:
time: 106 us
  Pallas kernels  101 us (95%)
  local copies, waits for them, and re-layouts  4.16 us (4%)
    pallas_call x1, Pallas kernels, on_device(): pl.pallas_call(functools.partial(kernel, n0), out_shape=(jax.ShapeDtypeSt...  101 us
    unnamed x10, local copies, waits for them, and re-layouts  4.16 us

profile of v3, /device:TPU:2, one launch (start us, length us, event | category | flops | bytes accessed | tf_op | source)
XLA Modules:
  0.0 106.2 jit_solution(2243658353027798098)
XLA Ops:
  0.6 101.4 %shard_map.102 = (bf16[2,4,64,128]{3,2,1,0:T(8,128)(2,1)}, bf16[2,4,64,128]{3,2,1,0:T(8,128)(2,1)}, bf16[128,512]{1,0:T(8,128)(2,1)}, bf16[128,512]{1,0:T(8,128)(2,1)}) custom-call(bf16[2,4,64,128]{3,2,1,0:T(8,128)(2,1)} %images.1, f32[7,7,128]{2,1,0:T(8,128)} %dwk.1, f32[1,128]{1,0:T(1,128)} %bitcast.4, bf16[128,512]{1,0:T(8,128)(2,1)} %w_in.1, ...), custom_call_target="tpu_custom_call" | custom-call | tf_op jit(solution)/shard_map/pallas_call | solution.py:640
  102.0 0.0 copy-start.2
  102.0 1.6 %copy.15 = bf16[2,4,64,128]{3,2,1,0:T(8,128)(2,1)} copy(bf16[2,4,64,128]{3,2,1,0:T(8,128)(2,1)} %get-tuple-element.8) | data formatting | bytes 262144
  103.6 0.0 copy-done.2
  103.6 0.0 copy-start.1
  103.6 0.7 copy.16
  104.3 0.3 copy-done.1
  104.6 0.0 copy-start
  104.6 0.7 copy.17
  105.2 0.3 copy-done
  105.5 0.7 copy.18
Async XLA Ops:
  102.0 1.6 %copy-start.2 = (bf16[2,4,64,128]{3,2,1,0:T(8,128)(2,1)S(1)}, bf16[2,4,64,128]{3,2,1,0:T(8,128)(2,1)}, u32[]{:S(2)}) copy-start(bf16[2,4,64,128]{3,2,1,0:T(8,128)(2,1)} %get-tuple-element.9) | copy-start | bytes 393220
  103.6 1.0 copy-start.1
  104.6 1.0 copy-start

commit v4 on v3

--- a/solution.py
+++ b/solution.py
@@ -18,10 +18,12 @@
 LEFT = 8
 TAP0 = LEFT - KS // 2
 N_SEND, N_RECV = 21, 165
-GATHER_ORDER = "gGWwxXSgGWwSxXgGWwSxXgGWwSxXgWwSx"
-BACK_ORDER = "mMBknNbBMcCbBNcCbBMcCbBNB"
-HALO_ORDER = "McCN"
-LAST_ORDER = "MNCC"
+PRE_ORDER = ""
+MID_ORDER = ""
+GATHER_ORDER = "gGWwxXSgGWwSxXgGWwSxXgGWwSxXgWwpSq012x34"
+BACK_ORDER = "mMBnNbBkMbBcCNbBcCMsbBNB"
+HALO_ORDER = "cCMN"
+LAST_ORDER = "cCMNCC"
 CONTRACT_LAST = (((1,), (1,)), ((), ()))
 CONTRACT_FIRST = (((0,), (0,)), ((), ()))
 
@@ -33,7 +35,7 @@
     pad, halo_lo, halo_hi, ghalo_lo, ghalo_hi, edge_lo, edge_hi,
     conv, normed, istd, tmp, st1, st2,
     cols, xg, xs, gg, wi, wo, hp, gh, hid, gpre,
-    gw, cb, bk, cb_m, cb_p, bk_m, bk_p, cb_mo, cb_po, bk_mo, bk_po,
+    less, gw, cb, bk, cb_m, cb_p, bk_m, bk_p, cb_mo, cb_po, bk_mo, bk_po,
     cb_x, bk_x, cb_xs, bk_xs, cb_xr, bk_xr, gs,
     g1, g2, g1_c, g2_c, g1_m, g1_p, g2_m, g2_p, g1_r, g2_r,
     send_sem, recv_sem,
@@ -88,6 +90,10 @@
     def blocks15():
         return group(xg.at[0:15])
 
+    barrier = pltpu.get_barrier_semaphore()
+    peers = [strip_up, strip_down, y_up, y_down, x_near, x_far, z_up, z_down]
+    for peer in peers:
+        pl.semaphore_signal(barrier, inc=1, device_id=peer, device_id_type=MESH)
     zero_edge = jnp.zeros((2, 10, LEFT, CB), F32)
     pad[:, :, 0:LEFT] = zero_edge
     pad[:, :, LEFT + 64 : 2 * LEFT + 64] = zero_edge
@@ -97,11 +103,6 @@
         gg[col, part] = (cot[part].astype(F32) * lscale[...]).astype(BF16)
     wi[core, y, xlo] = w_in[...]
     wo[core, y, xlo] = w_out[...]
-
-    barrier = pltpu.get_barrier_semaphore()
-    peers = [strip_up, strip_down, y_up, y_down, x_near, x_far, z_up, z_down]
-    for peer in peers:
-        pl.semaphore_signal(barrier, inc=1, device_id=peer, device_id_type=MESH)
     pl.semaphore_wait(barrier, len(peers))
 
     def ring_gather(buf, half, count, sem):
@@ -393,6 +394,14 @@
     wout = gather_row(wo, w_out)
     next(wout)
 
+    streams = dict(G=grads, g=grads2, W=win, w=wout)
+
+    def run(order):
+        for name in order:
+            next(streams[name])
+
+    run(PRE_ORDER)
+
     for copy in copies:
         copy.wait_recv()
     set_halo(halo_lo, halo_hi)
@@ -406,6 +415,7 @@
         put_sums(bh, mean, jnp.sum(dev * dev, axis=1, keepdims=True))
 
     taps_sum(False, after_conv)
+    run(MID_ORDER)
     pix, pix2, pix_rest = gather_col(xg)
     st1[0, 0, 0:8] = packed_sums()
     st1[0, 0, 8:16] = jnp.broadcast_to(gain[...], (8, CB))
@@ -427,40 +437,22 @@
         else:
             acc[...] += term
 
-    def normalise(step):
-        for other in (0, 1):
-            slot = (step % NZ, other)
-            half = xhi if other == 0 else 1 - xhi
-            place = slot[0] * 2 + other
-            scale = st1[slot[0], other, 8:9]
-            for q in range(4):
-                part = slice(q * 128, (q + 1) * 128)
-                dev = xg[at_z(step) * 2 + half, part].astype(F32)
-                value = (dev + cols[q, :, place : place + 1]) * istd[part] * scale
-                xs[at_z(step) * 2 + half, part] = value.astype(BF16)
-
-    streams = dict(G=grads, g=grads2, X=pix, x=pix2, W=win, w=wout, S=stats)
-    for name in GATHER_ORDER:
-        next(streams[name])
-    every = st1[...]
-    means, devs = every[:, :, 0:4], every[:, :, 4:8]
-    mean = jnp.sum(means, axis=(0, 1)) * (1.0 / 16)
-    shift = means - mean[None, None]
-    var = (jnp.sum(devs, axis=(0, 1)) + CB * jnp.sum(shift * shift, axis=(0, 1))) * (1.0 / C)
-    inv = lax.rsqrt(var + 1e-06)
-    for q in range(4):
-        part = slice(q * 128, (q + 1) * 128)
-        lines = [shift[o, i, q : q + 1] for o in range(NZ) for i in range(2)]
-        lines += [inv[q : q + 1], mean[q : q + 1], jnp.zeros((110, 128), F32)]
-        turned = jnp.transpose(jnp.concatenate(lines, axis=0))
-        cols[q] = turned
-        scale = jnp.broadcast_to(turned[:, 16:17], (128, CB))
-        istd[part] = scale
-        normed[part] = (conv[part] - turned[:, 17:18]) * scale
-    grads_rest(8)
-    product(gh, gg, wo, 0, True)
-    for step in (1, -1, 2, -2, 3, -3, 4):
-        product(gh, gg, wo, step, False)
+    def statistics():
+        every = st1[...]
+        means, devs = every[:, :, 0:4], every[:, :, 4:8]
+        mean = jnp.sum(means, axis=(0, 1)) * (1.0 / 16)
+        shift = means - mean[None, None]
+        var = (jnp.sum(devs, axis=(0, 1)) + CB * jnp.sum(shift * shift, axis=(0, 1))) * (1.0 / C)
+        inv = lax.rsqrt(var + 1e-06)
+        for q in range(4):
+            part = slice(q * 128, (q + 1) * 128)
+            lines = [shift[o, i, q : q + 1] for o in range(NZ) for i in range(2)]
+            lines += [inv[q : q + 1], mean[q : q + 1], jnp.zeros((110, 128), F32)]
+            turned = jnp.transpose(jnp.concatenate(lines, axis=0))
+            cols[q] = turned
+            scale = jnp.broadcast_to(turned[:, 16:17], (128, CB))
+            istd[part] = scale
+            normed[part] = (conv[part] - turned[:, 17:18]) * scale
 
     def gain_product(step, first):
         mine, theirs = st1[step % NZ, 0, 8:16], st1[step % NZ, 1, 8:16]
@@ -477,13 +469,49 @@
         else:
             gw[...] += term
 
-    for step in (0, 1, -1, 2, -2, 3, -3, 4):
-        gain_product(step, step == 0)
-    for count, steps in ((1, (0,)), (2, (1, -1)), (2, (2, -2)), (3, (3, -3, 4))):
-        pix_rest(count)
+    def normalise(step):
+        for other in (0, 1):
+            slot = (step % NZ, other)
+            half = xhi if other == 0 else 1 - xhi
+            place = slot[0] * 2 + other
+            scale = st1[slot[0], other, 8:9]
+            for q in range(4):
+                part = slice(q * 128, (q + 1) * 128)
+                dev = xg[at_z(step) * 2 + half, part].astype(F32)
+                value = (dev + cols[q, :, place : place + 1]) * istd[part] * scale
+                xs[at_z(step) * 2 + half, part] = value.astype(BF16)
+
+    around = (0, 1, -1, 2, -2, 3, -3, 4)
+
+    def grad_hidden():
+        grads_rest(8)
+        for step in around:
+            product(gh, gg, wo, step, step == 0)
+
+    def finish_stats():
+        statistics()
+        for step in around:
+            gain_product(step, step == 0)
+
+    def pre_activation(distance):
+        steps = around[max(0, 2 * distance - 1) : 2 * distance + 1]
+        pix_rest(len(steps))
         for step in steps:
             normalise(step)
             product(hp, xs, wi, step, step == 0)
+
+    def run(order):
+        work = {"p": grad_hidden, "q": finish_stats}
+        for name in order:
+            if name in "01234":
+                pre_activation(int(name))
+            elif name in work:
+                work[name]()
+            else:
+                next(streams[name])
+
+    streams.update(X=pix, x=pix2, S=stats)
+    run(GATHER_ORDER)
 
     def activate(i, carry):
         part = pl.ds(pl.multiple_of(i * 64, 64), 64)
@@ -555,18 +583,25 @@
                 weight_grad(g2, gg, hid)
             elif name == "n":
                 weight_grad(g1, xs, gpre)
+            elif name == "s":
+                norm_terms()
             else:
                 next(streams[name])
 
+    def norm_terms():
+        totals.wait_recv()
+        total = jnp.sum(st2[...], axis=0) * (1.0 / C)
+        for q in range(4):
+            part = slice(q * 128, (q + 1) * 128)
+            less[part] = istd[part] * (
+                spread(total[q : q + 1]) + normed[part] * spread(total[4 + q : 5 + q])
+            )
+
     run(BACK_ORDER)
 
-    totals.wait_recv()
-    total = jnp.sum(st2[...], axis=0) * (1.0 / C)
     for q in range(4):
         part = slice(q * 128, (q + 1) * 128)
-        value = istd[part] * (
-            gs[part] * gain[...] - spread(total[q : q + 1]) - normed[part] * spread(total[4 + q : 5 + q])
-        )
+        value = istd[part] * (gs[part] * gain[...]) - less[part]
         image, line = q // 2, 2 * (q % 2)
         value = value.reshape(2, 64, CB)
         pad[image, 3 + line : 5 + line, LEFT : LEFT + 64] = value
@@ -607,6 +642,11 @@
         assert next(stream, None) is None, name
 
 
+def hand_out(*refs):
+    for i in range(4):
+        refs[4 + i][...] = refs[i][...]
+
+
 def on_device(images, dw_kernel, norm_gain, proj_in, proj_out, layer_scale, cotangent):
     n0 = 256
     n1 = PIX - n0
@@ -623,7 +663,7 @@
         + [row_blocks] * 2
         + [vmem((PIX, HB), F32)] * 2
         + [vmem((PIX, HB), BF16)] * 2
-        + [vmem((8, HB), F32)]
+        + [vmem((PIX, CB), F32), vmem((8, HB), F32)]
         + [col_blocks] * 2
         + [vmem((4, PIX, CB), BF16)] * 4
         + [vmem((4, n0, CB), BF16)] * 4
@@ -637,7 +677,7 @@
         + [pltpu.SemaphoreType.DMA((N_SEND,)), pltpu.SemaphoreType.DMA((N_RECV,))]
     )
     block = pl.BlockSpec(memory_space=pltpu.VMEM)
-    return pl.pallas_call(
+    outs = pl.pallas_call(
         functools.partial(kernel, n0),
         out_shape=(
             jax.ShapeDtypeStruct(strip, BF16),
@@ -660,6 +700,12 @@
         layer_scale.reshape(1, CB),
         cotangent.reshape(PIX, CB),
     )
+    return pl.pallas_call(
+        hand_out,
+        out_shape=tuple(jax.ShapeDtypeStruct(out.shape, out.dtype) for out in outs),
+        in_specs=[block] * 4,
+        out_specs=(block,) * 4,
+    )(*outs)
 
 
 def solution(mesh):

time: 106 us -> 99.7 us (0.941)
  local copies, waits for them, and re-layouts: 4.16 us -> 0 us
  Pallas kernels: 101 us -> 98.7 us
    pallas_call x1, Pallas kernels: 101 us -> 96.8 us  [on_device(): pl.pallas_call(functools.partial(kernel, n0), out_shape=(jax.ShapeDtypeSt...]
    unnamed x10 -> x0, local copies, waits for them, and re-layouts: 4.16 us -> none
    pallas_call x0 -> x1, Pallas kernels: none -> 1.89 us  [on_device(): pl.pallas_call(hand_out, out_shape=tuple((jax.ShapeDtypeStruct(out.shape,...]
where the time goes in v4:
time: 99.7 us; the launch traced here: 99.3 us
  Pallas kernels  98.7 us (99%)
    pallas_call x1, Pallas kernels, on_device(): pl.pallas_call(functools.partial(kernel, n0), out_shape=(jax.ShapeDtypeSt...  96.8 us

profile of v4, /device:TPU:2, one launch (start us, length us, event | category | flops | bytes accessed | tf_op | source)
XLA Modules:
  0.0 99.3 jit_solution(17350995192138263820)
XLA Ops:
  0.6 96.8 %shard_map.102 = (bf16[2,4,64,128]{3,2,1,0:T(8,128)(2,1)}, bf16[2,4,64,128]{3,2,1,0:T(8,128)(2,1)}, bf16[128,512]{1,0:T(8,128)(2,1)}, bf16[128,512]{1,0:T(8,128)(2,1)}) custom-call(bf16[2,4,64,128]{3,2,1,0:T(8,128)(2,1)} %images.1, f32[7,7,128]{2,1,0:T(8,128)} %dwk.1, f32[1,128]{1,0:T(1,128)} %bitcast.4, bf16[128,512]{1,0:T(8,128)(2,1)} %w_in.1, ...), custom_call_target="tpu_custom_call" | custom-call | tf_op jit(solution)/shard_map/pallas_call | solution.py:680
  97.4 1.9 %shard_map.103 = (bf16[2,4,64,128]{3,2,1,0:T(8,128)(2,1)}, bf16[2,4,64,128]{3,2,1,0:T(8,128)(2,1)}, bf16[128,512]{1,0:T(8,128)(2,1)}, bf16[128,512]{1,0:T(8,128)(2,1)}) custom-call(bf16[2,4,64,128]{3,2,1,0:T(8,128)(2,1)} %get-tuple-element.8.refs_0_, bf16[2,4,64,128]{3,2,1,0:T(8,128)(2,1)} %get-tuple-element.9.refs_1_, ...), custom_call_target="tpu_custom_call" | custom-call | tf_op jit(solution)/shard_map/pallas_call | solution.py:703

commit v5 on v4

--- a/solution.py
+++ b/solution.py
@@ -20,7 +20,7 @@
 N_SEND, N_RECV = 21, 165
 PRE_ORDER = ""
 MID_ORDER = ""
-GATHER_ORDER = "gGWwxXSgGWwSxXgGWwSxXgGWwSxXgWwpSq012x34"
+GATHER_ORDER = "gGxXSgGSxXWwgGWwSxXWwgGWwSxXgWwpSq012x34"
 BACK_ORDER = "mMBnNbBkMbBcCNbBcCMsbBNB"
 HALO_ORDER = "cCMN"
 LAST_ORDER = "cCMNCC"
@@ -389,21 +389,21 @@
         send(images.at[:, 0:3], halo_hi, strip_down),
     ]
     grads, grads2, grads_rest = gather_col(gg)
+    streams = dict(G=grads, g=grads2)
+
+    def run(order):
+        for name in order:
+            next(streams[name])
+
+    run(PRE_ORDER)
+
+    for copy in copies:
+        copy.wait_recv()
     win = gather_row(wi, w_in)
     next(win)
     wout = gather_row(wo, w_out)
     next(wout)
-
-    streams = dict(G=grads, g=grads2, W=win, w=wout)
-
-    def run(order):
-        for name in order:
-            next(streams[name])
-
-    run(PRE_ORDER)
-
-    for copy in copies:
-        copy.wait_recv()
+    streams.update(W=win, w=wout)
     set_halo(halo_lo, halo_hi)
 
     def after_conv(bh, total):
@@ -648,7 +648,7 @@
 
 
 def on_device(images, dw_kernel, norm_gain, proj_in, proj_out, layer_scale, cotangent):
-    n0 = 256
+    n0 = 224
     n1 = PIX - n0
     strip = images.shape
     vmem = pltpu.VMEM

time: 99.7 us -> 98.7 us (0.990)
  no operation moved by 1% of the time
where the time goes in v5:
time: 98.7 us; the launch traced here: 98.6 us
  Pallas kernels  98 us (99%)
    pallas_call x1, Pallas kernels, on_device(): pl.pallas_call(functools.partial(kernel, n0), out_shape=(jax.ShapeDtypeSt...  96.1 us

profile of v5, /device:TPU:2, one launch (start us, length us, event | category | flops | bytes accessed | tf_op | source)
XLA Modules:
  0.0 98.6 jit_solution(18231118415820662764)
XLA Ops:
  0.6 96.1 %shard_map.102 = (bf16[2,4,64,128]{3,2,1,0:T(8,128)(2,1)}, bf16[2,4,64,128]{3,2,1,0:T(8,128)(2,1)}, bf16[128,512]{1,0:T(8,128)(2,1)}, bf16[128,512]{1,0:T(8,128)(2,1)}) custom-call(bf16[2,4,64,128]{3,2,1,0:T(8,128)(2,1)} %images.1, f32[7,7,128]{2,1,0:T(8,128)} %dwk.1, f32[1,128]{1,0:T(1,128)} %bitcast.4, bf16[128,512]{1,0:T(8,128)(2,1)} %w_in.1, ...), custom_call_target="tpu_custom_call" | custom-call | tf_op jit(solution)/shard_map/pallas_call | solution.py:680
  96.7 1.9 %shard_map.103 = (bf16[2,4,64,128]{3,2,1,0:T(8,128)(2,1)}, bf16[2,4,64,128]{3,2,1,0:T(8,128)(2,1)}, bf16[128,512]{1,0:T(8,128)(2,1)}, bf16[128,512]{1,0:T(8,128)(2,1)}) custom-call(bf16[2,4,64,128]{3,2,1,0:T(8,128)(2,1)} %get-tuple-element.8.refs_0_, bf16[2,4,64,128]{3,2,1,0:T(8,128)(2,1)} %get-tuple-element.9.refs_1_, ...), custom_call_target="tpu_custom_call" | custom-call | tf_op jit(solution)/shard_map/pallas_call | solution.py:703

commit v6 on v5

--- a/solution.py
+++ b/solution.py
@@ -23,7 +23,8 @@
 GATHER_ORDER = "gGxXSgGSxXWwgGWwSxXWwgGWwSxXgWwpSq012x34"
 BACK_ORDER = "mMBnNbBkMbBcCNbBcCMsbBNB"
 HALO_ORDER = "cCMN"
-LAST_ORDER = "cCMNCC"
+MIDDLE_ORDER = "cC"
+LAST_ORDER = "MNCC"
 CONTRACT_LAST = (((1,), (1,)), ((), ()))
 CONTRACT_FIRST = (((0,), (0,)), ((), ()))
 
@@ -617,6 +618,7 @@
     for copy in copies:
         copy.wait_recv()
     set_halo(ghalo_lo, ghalo_hi)
+    run(MIDDLE_ORDER)
 
     def after_transposed(bh, total):
         part = pl.ds(pl.multiple_of(bh * 64, 64), 64)

time: 98.7 us -> 98.6 us (level)
  no operation moved by 1% of the time
where the time goes in v6:
time: 98.6 us; the launch traced here: 98.5 us
  Pallas kernels  97.8 us (99%)
    pallas_call x1, Pallas kernels, on_device(): pl.pallas_call(functools.partial(kernel, n0), out_shape=(jax.ShapeDtypeSt...  95.9 us

profile of v6, /device:TPU:2, one launch (start us, length us, event | category | flops | bytes accessed | tf_op | source)
XLA Modules:
  0.0 98.5 jit_solution(670359900156973711)
XLA Ops:
  0.6 95.9 %shard_map.102 = (bf16[2,4,64,128]{3,2,1,0:T(8,128)(2,1)}, bf16[2,4,64,128]{3,2,1,0:T(8,128)(2,1)}, bf16[128,512]{1,0:T(8,128)(2,1)}, bf16[128,512]{1,0:T(8,128)(2,1)}) custom-call(bf16[2,4,64,128]{3,2,1,0:T(8,128)(2,1)} %images.1, f32[7,7,128]{2,1,0:T(8,128)} %dwk.1, f32[1,128]{1,0:T(1,128)} %bitcast.4, bf16[128,512]{1,0:T(8,128)(2,1)} %w_in.1, ...), custom_call_target="tpu_custom_call" | custom-call | tf_op jit(solution)/shard_map/pallas_call | solution.py:682
  96.6 1.9 %shard_map.103 = (bf16[2,4,64,128]{3,2,1,0:T(8,128)(2,1)}, bf16[2,4,64,128]{3,2,1,0:T(8,128)(2,1)}, bf16[128,512]{1,0:T(8,128)(2,1)}, bf16[128,512]{1,0:T(8,128)(2,1)}) custom-call(bf16[2,4,64,128]{3,2,1,0:T(8,128)(2,1)} %get-tuple-element.8.refs_0_, bf16[2,4,64,128]{3,2,1,0:T(8,128)(2,1)} %get-tuple-element.9.refs_1_, ...), custom_call_target="tpu_custom_call" | custom-call | tf_op jit(solution)/shard_map/pallas_call | solution.py:705
